TPU v7x, 256 devices: a whole 4x4x8 slice. The times are simulated.
256 devices in a mesh: cp: 32 (over x_lo, z, core), tp: 8 (over y, x_hi).
Axes of the slice: x: 4 (x_hi: 2, x_lo: 2; x = x_hi * 2 + x_lo), y: 4, z: 8, core: 2. Of those that a mesh axis runs over, the one named last changes fastest.
Arguments:
- query: bfloat16 [2048, 16384], P(('cp', 'tp')), may hold values from -6 to 6
- fresh_key_rows: bfloat16 [2048, 1024], P(('cp', 'tp')), may hold values from -6 to 6
- fresh_value_rows: bfloat16 [2048, 1024], P(('cp', 'tp')), may hold values from -6 to 6
- cached_key_rows: bfloat16 [16384, 1024], P('cp', 'tp'), may hold values from -6 to 6
- cached_value_rows: bfloat16 [16384, 1024], P('cp', 'tp'), may hold values from -6 to 6
- prefix_len: int32 [1], replicated, may hold values from 8192 to 16384
- stripe_owner: int32 [32], replicated, may hold values from 0 to 31, each once
Outputs:
- attended: bfloat16 [2048, 16384], P('cp', 'tp')
Inputs may be any that keep to these rules, and one draw needn't show every extreme that they name: `stripe_owner`: a permutation of 0 to 31.
All inputs are finite; a program needn't handle non-finite values.
Results may differ from a plain program's by a relative error of at most 0.0075.
Values may be sent and summed in bfloat16 or wider, within the bound.
No kernel may reach another device: no remote copies, remote signals or barrier semaphores. Data moves between devices by JAX's collectives and lax.ppermute only.
A program may use at most 64 MiB of HBM per device.

v0:
```python
import functools

import jax
import jax.numpy as jnp
from jax import lax
from jax.experimental import pallas as pl
from jax.experimental.pallas import tpu as pltpu
from jax.sharding import Mesh
from jax.sharding import PartitionSpec as P

HEAD_SIZE = 128
NEG = -1e30
SCALE2 = HEAD_SIZE ** (-0.5) * 1.4426950408889634
GROUP = 8
BLOCK = 512
PARTS = 4

bf16 = jnp.bfloat16
f32 = jnp.float32


def attend_kernel(n_cached, has_fresh, first, last, rows, heads, *refs):
    info = refs[0]
    at = 1
    cached = refs[at : at + n_cached]
    at += n_cached
    q_ref = refs[at]
    at += 1
    if has_fresh:
        fresh_ref, fresh_mask = refs[at : at + 2]
        at += 2
    if not first:
        m_in, l_in, acc_in = refs[at : at + 3]
        at += 3
    if last:
        keep_ref, send_ref, lse_ref = refs[at : at + 3]
        at += 3
    else:
        m_ref, l_ref, acc_ref = refs[at : at + 3]
        at += 3
    kbuf, vbuf, qbuf, s_even, s_odd, p_even, p_odd, sems = refs[at : at + 8]
    at += 8
    if last:
        m_ref, l_ref, acc_ref = refs[at : at + 3]
    groups = heads // GROUP
    wide = GROUP * rows
    plen = info[0]

    def copies(i, slot):
        row = pl.multiple_of(slot * BLOCK, BLOCK)
        return (
            pltpu.make_async_copy(
                cached[i].at[pl.ds(0, BLOCK), :], kbuf.at[pl.ds(row, BLOCK), pl.ds(0, HEAD_SIZE)], sems.at[i]
            ),
            pltpu.make_async_copy(cached[i].at[pl.ds(BLOCK, BLOCK), :], vbuf.at[pl.ds(row, BLOCK), :], sems.at[i]),
        )

    def visit(action):
        slot = jnp.int32(0)
        for i in range(n_cached):
            live = info[1 + i] < plen

            @pl.when(live)
            def _(slot=slot, i=i):
                action(i, slot)

            slot = slot + live.astype(jnp.int32)
        return slot

    def begin(i, slot):
        one, two = copies(i, slot)
        one.start()
        two.start()

    used = visit(begin)

    eye = (
        lax.broadcasted_iota(jnp.int32, (rows, HEAD_SIZE), 0) == lax.broadcasted_iota(jnp.int32, (rows, HEAD_SIZE), 1)
    ).astype(bf16)
    for h in range(heads):
        qbuf[pl.ds(h * rows, rows), 0:HEAD_SIZE] = q_ref[:, h * HEAD_SIZE : (h + 1) * HEAD_SIZE]
        qbuf[pl.ds(h * rows, rows), HEAD_SIZE : 2 * HEAD_SIZE] = eye

    def bias(i, slot):
        spot = lax.broadcasted_iota(jnp.int32, (BLOCK, HEAD_SIZE), 0) + info[1 + i]
        kbuf[pl.ds(pl.multiple_of(slot * BLOCK, BLOCK), BLOCK), pl.ds(HEAD_SIZE, HEAD_SIZE)] = jnp.where(
            spot < plen, 0.0, NEG
        ).astype(bf16)

    visit(bias)
    if has_fresh:
        sources, per = fresh_ref.shape[0], fresh_ref.shape[2]
        count = sources * per
        base = pl.multiple_of(used * BLOCK, BLOCK)
        kbuf[pl.ds(base, count), pl.ds(0, HEAD_SIZE)] = fresh_ref[:, 0].reshape(count, HEAD_SIZE)
        vbuf[pl.ds(base, count), :] = fresh_ref[:, 1].reshape(count, HEAD_SIZE)
        kbuf[pl.ds(base, count), pl.ds(HEAD_SIZE, HEAD_SIZE)] = fresh_mask[...]
        used = used + count // BLOCK

    if first:
        m_ref[...] = jnp.full_like(m_ref, NEG)
        l_ref[...] = jnp.zeros_like(l_ref)
        acc_ref[...] = jnp.zeros_like(acc_ref)
    else:
        m_ref[...] = m_in[...]
        l_ref[...] = l_in[...]
        acc_ref[...] = acc_in[...]

    def finish(i, slot):
        one, two = copies(i, slot)
        one.wait()
        two.wait()

    visit(finish)

    piece = wide // PARTS
    spans = [slice(j * piece, (j + 1) * piece) for j in range(PARTS)]

    def at_block(buf, b):
        return buf[pl.ds(pl.multiple_of(b * BLOCK, BLOCK), BLOCK), :]

    def qk(g, b, j):
        q = qbuf[pl.ds(pl.multiple_of(g * wide + j * piece, piece), piece), :]
        return lax.dot_general(at_block(kbuf, b), q, (((1,), (1,)), ((), ())), preferred_element_type=f32)

    def pv(b, p):
        return lax.dot_general(at_block(vbuf, b), p, (((0,), (0,)), ((), ())), preferred_element_type=f32)

    def after(g, b):
        end = b + 1 == used
        return jnp.where(end, g + 1, g), jnp.where(end, 0, b + 1)

    def turn(carry, s_now, p_now, s_next, p_before):
        g0, b0, old, g, b = carry
        gn, bn = after(g, b)
        factors = []
        for j, span in enumerate(spans):
            s_next[:, span] = qk(jnp.minimum(gn, groups - 1), bn, j)
            s = s_now[:, span]
            m = m_ref[g, :, span]
            new = jnp.maximum(m, jnp.max(s, axis=0, keepdims=True))
            factor = jnp.exp2((m - new) * SCALE2)
            p = jnp.exp2((s - new) * SCALE2)
            m_ref[g, :, span] = new
            l_ref[g, :, span] = l_ref[g, :, span] * factor + jnp.sum(p, axis=0, keepdims=True)
            p_now[:, span] = p.astype(bf16)
            acc_ref[g0, :, span] = acc_ref[g0, :, span] * old[j] + pv(b0, p_before[:, span])
            factors.append(factor)
        return g, b, tuple(factors), gn, bn

    zero = jnp.int32(0)
    p_odd[...] = jnp.zeros_like(p_odd)
    for j, span in enumerate(spans):
        s_even[:, span] = qk(zero, zero, j)

    def body(_, carry):
        carry = turn(carry, s_even, p_even, s_odd, p_odd)
        return turn(carry, s_odd, p_odd, s_even, p_even)

    ones = tuple(jnp.ones((1, piece), f32) for _ in range(PARTS))
    g0, b0, old, _, _ = lax.fori_loop(0, groups * used // 2, body, (zero, zero, ones, zero, zero))
    for j, span in enumerate(spans):
        acc_ref[g0, :, span] = acc_ref[g0, :, span] * old[j] + pv(b0, p_odd[:, span])

    if last:
        half = rows // 2
        for g in range(groups):
            total = l_ref[g]
            lse = m_ref[g] * SCALE2 + jnp.log2(total)
            out = (acc_ref[g] / total).T
            for j in range(GROUP):
                h = g * GROUP + j
                own = out[j * rows : (j + 1) * rows]
                keep_ref[:, h * HEAD_SIZE : (h + 1) * HEAD_SIZE] = own[:half]
                send_ref[:, h * HEAD_SIZE : (h + 1) * HEAD_SIZE] = own[half:].astype(bf16)
                lse_ref[h : h + 1, :] = lse[:, j * rows : (j + 1) * rows]


def attend(info, cached, queries, heads, fresh=None, state=None, last=False):
    rows = queries.shape[0]
    wide = GROUP * rows
    groups = heads // GROUP
    first = state is None
    n_cached = len(cached)
    slots = n_cached + (0 if fresh is None else fresh[0].shape[0] * fresh[0].shape[2] // BLOCK)
    vm = pl.BlockSpec(memory_space=pltpu.VMEM)
    args = [info, *cached, queries]
    specs = [pl.BlockSpec(memory_space=pltpu.SMEM)] + [pl.BlockSpec(memory_space=pl.ANY)] * n_cached + [vm]
    if fresh is not None:
        args += list(fresh)
        specs += [vm, vm]
    if not first:
        args += list(state)
        specs += [vm] * 3
    states = [
        ((groups, 1, wide), f32),
        ((groups, 1, wide), f32),
        ((groups, HEAD_SIZE, wide), f32),
    ]
    if last:
        outs = [
            jax.ShapeDtypeStruct((rows // 2, heads * HEAD_SIZE), f32),
            jax.ShapeDtypeStruct((rows // 2, heads * HEAD_SIZE), bf16),
            jax.ShapeDtypeStruct((heads, rows), f32),
        ]
    else:
        outs = [jax.ShapeDtypeStruct(s, d) for s, d in states]
    scratch = [
        pltpu.VMEM((slots * BLOCK, 2 * HEAD_SIZE), bf16),
        pltpu.VMEM((slots * BLOCK, HEAD_SIZE), bf16),
        pltpu.VMEM((heads * rows, 2 * HEAD_SIZE), bf16),
        pltpu.VMEM((BLOCK, wide), f32),
        pltpu.VMEM((BLOCK, wide), f32),
        pltpu.VMEM((BLOCK, wide), bf16),
        pltpu.VMEM((BLOCK, wide), bf16),
        pltpu.SemaphoreType.DMA((max(n_cached, 1),)),
    ]
    if last:
        scratch += [pltpu.VMEM(s, d) for s, d in states]
    return pl.pallas_call(
        functools.partial(attend_kernel, n_cached, fresh is not None, first, last, rows, heads),
        out_shape=outs,
        in_specs=specs,
        out_specs=[vm] * 3,
        scratch_shapes=scratch,
        compiler_params=pltpu.CompilerParams(vmem_limit_bytes=40 * 2**20),
        cost_estimate=pl.CostEstimate(
            flops=4 * slots * BLOCK * heads * rows * HEAD_SIZE * 2,
            bytes_accessed=slots * BLOCK * HEAD_SIZE * 4,
            transcendentals=slots * BLOCK * heads * rows,
        ),
    )(*args)


def merge_kernel(heads, keep_ref, got_ref, mine_ref, theirs_ref, out_ref):
    half = keep_ref.shape[0]
    mine = mine_ref[...].T[:half]
    theirs = theirs_ref[...].T[half:]
    peak = jnp.maximum(mine, theirs)
    one = jnp.exp2(mine - peak)
    two = jnp.exp2(theirs - peak)
    total = one + two
    one = one / total
    two = two / total
    for h in range(heads):
        cols = slice(h * HEAD_SIZE, (h + 1) * HEAD_SIZE)
        out_ref[:, cols] = (
            keep_ref[:, cols] * one[:, h : h + 1] + got_ref[:, cols].astype(f32) * two[:, h : h + 1]
        ).astype(bf16)


def merge(heads, keep, got, mine, theirs):
    return pl.pallas_call(
        functools.partial(merge_kernel, heads),
        out_shape=jax.ShapeDtypeStruct(keep.shape, bf16),
        in_specs=[pl.BlockSpec(memory_space=pltpu.VMEM)] * 4,
        out_specs=pl.BlockSpec(memory_space=pltpu.VMEM),
    )(keep, got, mine, theirs)


def step(query, fresh_key_rows, fresh_value_rows, cached_key_rows, cached_value_rows, prefix_len, stripe_owner):
    nx, nz, nc, ntp = (lax.axis_size(a) for a in ("x", "z", "c", "tp"))
    x, z, c = (lax.axis_index(a) for a in ("x", "z", "c"))
    parts = nx * nz * nc
    up = [(i, (i + 1) % nz) for i in range(nz)]
    down = [(i, (i - 1) % nz) for i in range(nz)]
    swap = [(0, 1), (1, 0)]

    own = jnp.concatenate([cached_key_rows, cached_value_rows], axis=0)
    other = lax.ppermute(own, "x", swap)

    def hop(above, below):
        return (
            (lax.ppermute(above[0], "z", up), lax.ppermute(above[1], "z", up)),
            (lax.ppermute(below[0], "z", down), lax.ppermute(below[1], "z", down)),
        )

    up1, down1 = hop((own, other), (own, other))
    up2, down2 = hop(up1, down1)

    local = query.shape[0]
    width = query.shape[1] // ntp
    mixed = jnp.concatenate(
        [
            query.reshape(local, ntp, width),
            fresh_key_rows.reshape(local, ntp, HEAD_SIZE),
            fresh_value_rows.reshape(local, ntp, HEAD_SIZE),
        ],
        axis=2,
    ).reshape(local, ntp * (width + 2 * HEAD_SIZE))
    mixed = lax.all_to_all(mixed, "tp", split_axis=1, concat_axis=0, tiled=True)
    rows = mixed.shape[0]
    stripe = rows // parts
    heads = width // HEAD_SIZE
    order = jnp.arange(parts, dtype=jnp.int32)
    inverse = jnp.sum(jnp.where(stripe_owner[None, :] == order[:, None], order[None, :], 0), axis=1)
    row_of = (inverse[:, None] * stripe + jnp.arange(stripe, dtype=jnp.int32)[None, :]).reshape(rows)
    pick = (row_of[:, None] == jnp.arange(rows, dtype=jnp.int32)[None, :]).astype(bf16)
    arranged = jnp.dot(pick, mixed[:, :width], preferred_element_type=f32).astype(bf16)
    mine = lax.all_to_all(arranged, ("x", "z"), split_axis=0, concat_axis=0, tiled=True)
    peers = lax.ppermute(mine, "c", swap)

    def spot(rel, s, src, i):
        part = (src != c).astype(jnp.int32)
        owner = jnp.where(rel == 0, c, 1 - c)
        return part * rows + (s * nc + owner) * stripe + i

    idx = jnp.arange(nc * rows, dtype=jnp.int32)
    i_, src_, s_, rel_ = idx % stripe, idx // stripe % nc, idx // (stripe * nc) % (nx * nz), idx // rows
    choose = (spot(rel_, s_, src_, i_)[:, None] == idx[None, :]).astype(bf16)
    queries = jnp.dot(choose, jnp.concatenate([mine, peers], axis=0), preferred_element_type=f32).astype(bf16)
    owner_ = (x * nz + z) * nc + jnp.where(rel_ == 0, c, 1 - c)
    residue_ = jnp.sum(jnp.where(owner_[:, None] == order[None, :], inverse[None, :], 0), axis=1)
    natural = (s_ * nc + src_) * rows + residue_ * stripe + i_

    fresh = jnp.concatenate(
        [mixed[:, width : width + HEAD_SIZE], mixed[:, width + HEAD_SIZE :]], axis=0
    ).reshape(1, 2, rows, HEAD_SIZE)
    key_id = jnp.arange(nx * nz * rows, dtype=jnp.int32)
    key_natural = (key_id // rows * nc + c) * rows + key_id % rows
    fresh_mask = jnp.where(key_natural[:, None] <= natural[None, :], 0.0, NEG).astype(bf16)

    slots = cached_key_rows.shape[0]

    def info_of(where):
        flip = jnp.array([w[0] for w in where], jnp.int32)
        step = jnp.array([w[1] + nz for w in where], jnp.int32)
        starts = ((jnp.where(flip == 0, x, 1 - x) * nz + (z + step) % nz) * nc + c) * slots
        return jnp.concatenate([prefix_len, starts.astype(jnp.int32)])

    def around(step):
        return [(0, -step), (1, -step), (0, step), (1, step)]

    first_info = info_of([(0, 0), (1, 0)] + around(1))
    state = attend(first_info, [own, other, *up1, *down1], queries, heads)
    up2, down2, state = lax.optimization_barrier((up2, down2, state))
    up3, down3 = hop(up2, down2)
    fresh, state = lax.optimization_barrier((fresh, state))
    fresh = jnp.broadcast_to(fresh, (nx * nz, 2, rows, HEAD_SIZE))
    fresh = lax.all_to_all(fresh, ("x", "z"), split_axis=0, concat_axis=0, tiled=True)
    state = attend(info_of(around(2)), [*up2, *down2], queries, heads, state=state)
    up3, down3, state = lax.optimization_barrier((up3, down3, state))
    far_own = lax.ppermute(up3[0], "z", up)
    far_other = lax.ppermute(down3[1], "z", down)
    state = attend(info_of(around(3)), [*up3, *down3], queries, heads, state=state)
    keep, give, lse = attend(
        info_of([(0, 4), (1, 4)]),
        [far_own, far_other],
        queries,
        heads,
        fresh=(fresh, fresh_mask),
        state=state,
        last=True,
    )
    got = lax.ppermute(give, "c", swap)
    their_lse = lax.ppermute(lse, "c", swap)
    return merge(heads, keep, got, lse, their_lse)


def solution(mesh):
    devices = mesh.devices
    parts = Mesh(devices.reshape(2, devices.shape[0] // 4, 2, devices.shape[1]), ("x", "z", "c", "tp"))
    rows = ("x", "z", "c", "tp")
    cp = ("x", "z", "c")
    return jax.shard_map(
        step,
        mesh=parts,
        in_specs=(P(rows, None), P(rows, None), P(rows, None), P(cp, "tp"), P(cp, "tp"), P(), P()),
        out_specs=P(cp, "tp"),
        check_vma=False,
    )
```

profile of v0, /device:TPU:1, one launch (start us, length us, event | category | flops | bytes accessed | tf_op | source)
XLA Modules:
  0.0 112.1 jit_solution(358773292297870911)
XLA Ops:
  0.0 1.0 constant_dynamic-update-slice_fusion.1
  1.0 0.0 copy-start.7
  1.0 0.0 copy-start.8
  1.0 2.1 %collective-permute-start.2 = (bf16[1024,128]{1,0:T(8,128)(2,1)S(1)}, bf16[1024,128]{1,0:T(8,128)(2,1)S(1)}, u32[]{:S(2)}, u32[]{:S(2)}) collective-permute-start(bf16[1024,128]{1,0:T(8,128)(2,1)S(1)} %constant_dynamic-update-slice_fusion.refs_1_), channel_id=1, source_target_pairs={{0,128},{128,0},{1,129},{129,1},{2,130},{130,2},{3,131},{131,3},{4... | collective-permute-start | bytes 786440 | tf_op jit(solution)/shard_map/ppermute | solution.py:270
  3.1 1.6 %collective-permute-start = (bf16[1024,128]{1,0:T(8,128)(2,1)S(1)}, bf16[1024,128]{1,0:T(8,128)(2,1)S(1)}, u32[]{:S(2)}, u32[]{:S(2)}) collective-permute-start(bf16[1024,128]{1,0:T(8,128)(2,1)S(1)} %constant_dynamic-update-slice_fusion.refs_1_), channel_id=1, source_target_pairs={{0,16},{16,32},{32,48},{48,64},{64,80},{80,96},{96,112},{112,0},{1... | collective-permute-start | bytes 786440 | tf_op jit(solution)/shard_map/ppermute | solution.py:274
  4.8 3.9 %collective-permute-start.5 = (bf16[1024,128]{1,0:T(8,128)(2,1)S(1)}, bf16[1024,128]{1,0:T(8,128)(2,1)S(1)}, u32[]{:S(2)}, u32[]{:S(2)}) collective-permute-start(bf16[1024,128]{1,0:T(8,128)(2,1)S(1)} %constant_dynamic-update-slice_fusion.refs_1_), channel_id=1, source_target_pairs={{0,112},{16,0},{32,16},{48,32},{64,48},{80,64},{96,80},{112,96},{1... | collective-permute-start | bytes 786440 | tf_op jit(solution)/shard_map/ppermute | solution.py:275
  8.7 0.7 pad_maximum_fusion
  9.5 6.4 %all-to-all-start = ((bf16[8,8,2304]{2,0,1:T(8,128)(2,1)}), bf16[8,8,2304]{2,0,1:T(8,128)(2,1)S(1)}, u32[]{:S(2)}, u32[]{:S(2)}) async-start(bf16[8,8,2304]{2,0,1:T(8,128)(2,1)} %pad_maximum_fusion), calls=%async_computation | async-start | bytes 589824 | tf_op jit(solution)/shard_map/all_to_all | solution.py:291
  16.5 0.0 copy-start.15
  16.5 0.6 copy-done.15
  17.1 0.1 select_reduce_fusion.1
  17.3 0.1 iota_add_fusion
  17.4 0.6 copy-done.13
  18.0 0.0 copy-done.14
  18.0 0.6 copy-done.10
  18.7 0.0 copy-done.11
  18.7 0.0 copy-done.12
  18.7 0.1 pad_add_fusion.1.refs_0_
  18.8 0.1 add.276
  18.9 0.1 pad_add_fusion.2
  19.0 4.7 %all-to-all-done = bf16[8,8,2304]{2,0,1:T(8,128)(2,1)S(1)} async-done(((bf16[8,8,2304]{2,0,1:T(8,128)(2,1)}), bf16[8,8,2304]{2,0,1:T(8,128)(2,1)S(1)}, u32[]{:S(2)}, u32[]{:S(2)}) %all-to-all-start) | async-done | bytes 294944 | tf_op jit(solution)/shard_map/all_to_all | solution.py:291
  23.6 0.3 convolution_convert_fusion.1
  23.9 0.8 all_to_all.26
  24.7 5.5 %all-to-all-start.1 = ((bf16[16,4,2048]{2,1,0:T(4,128)(2,1)}), bf16[16,4,2048]{2,1,0:T(4,128)(2,1)S(1)}, u32[]{:S(2)}, u32[]{:S(2)}) async-start(bf16[16,4,2048]{2,1,0:T(4,128)(2,1)} %all_to_all.26), calls=%async_computation.1 | async-start | bytes 524288 | tf_op jit(solution)/shard_map/all_to_all | solution.py:300
  30.3 0.1 select_reduce_fusion
  30.4 0.1 pad_add_fusion.refs_0_
  30.5 1.4 %collective-permute-start.3 = (bf16[1024,128]{1,0:T(8,128)(2,1)S(1)}, bf16[1024,128]{1,0:T(8,128)(2,1)S(1)}, u32[]{:S(2)}, u32[]{:S(2)}) collective-permute-start(bf16[1024,128]{1,0:T(8,128)(2,1)S(1)} %collective-permute-done.2.refs_2_), channel_id=1, source_target_pairs={{0,16},{16,32},{32,48},{48,64},{64,80},{80,96},{96,112},{112,0},{1... | collective-permute-start | bytes 786440 | tf_op jit(solution)/shard_map/ppermute | solution.py:274
  31.9 1.3 %collective-permute-start.7 = (bf16[1024,128]{1,0:T(8,128)(2,1)S(1)}, bf16[1024,128]{1,0:T(8,128)(2,1)S(1)}, u32[]{:S(2)}, u32[]{:S(2)}) collective-permute-start(bf16[1024,128]{1,0:T(8,128)(2,1)S(1)} %collective-permute-done.2.refs_2_), channel_id=1, source_target_pairs={{0,112},{16,0},{32,16},{48,32},{64,48},{80,64},{96,80},{112,96},{1... | collective-permute-start | bytes 786440 | tf_op jit(solution)/shard_map/ppermute | solution.py:275
  33.2 4.8 %all-to-all-done.1 = bf16[16,4,2048]{2,1,0:T(4,128)(2,1)S(1)} async-done(((bf16[16,4,2048]{2,1,0:T(4,128)(2,1)}), bf16[16,4,2048]{2,1,0:T(4,128)(2,1)S(1)}, u32[]{:S(2)}, u32[]{:S(2)}) %all-to-all-start.1) | async-done | bytes 262176 | tf_op jit(solution)/shard_map/all_to_all | solution.py:300
  38.0 0.1 all_to_all.28
  38.1 6.0 %collective-permute-start.9 = (bf16[64,2048]{1,0:T(8,128)(2,1)S(1)}, bf16[64,2048]{1,0:T(8,128)(2,1)S(1)}, u32[]{:S(2)}, u32[]{:S(2)}) collective-permute-start(bf16[64,2048]{1,0:T(8,128)(2,1)S(1)} %all_to_all.28), channel_id=1, source_target_pairs={{0,8},{8,0},{1,9},{9,1},{2,10},{10,2},{3,11},{11,3},{4,12},{12,4},... | collective-permute-start | bytes 786440 | tf_op jit(solution)/shard_map/ppermute | solution.py:301
  44.1 0.0 collective-permute-done.refs_3_
  44.1 0.6 collective-permute-start.1
  44.7 2.2 %collective-permute-start.6 = (bf16[1024,128]{1,0:T(8,128)(2,1)S(1)}, bf16[1024,128]{1,0:T(8,128)(2,1)S(1)}, u32[]{:S(2)}, u32[]{:S(2)}) collective-permute-start(bf16[1024,128]{1,0:T(8,128)(2,1)S(1)} %collective-permute-done.5.refs_5_), channel_id=1, source_target_pairs={{0,112},{16,0},{32,16},{48,32},{64,48},{80,64},{96,80},{112,96},{1... | collective-permute-start | bytes 786440 | tf_op jit(solution)/shard_map/ppermute | solution.py:275
  46.9 0.0 collective-permute-done.3.refs_4_
  46.9 0.0 collective-permute-start.4
  46.9 0.0 collective-permute-done.7.refs_6_
  46.9 2.7 %collective-permute-start.8 = (bf16[1024,128]{1,0:T(8,128)(2,1)S(1)}, bf16[1024,128]{1,0:T(8,128)(2,1)S(1)}, u32[]{:S(2)}, u32[]{:S(2)}) collective-permute-start(bf16[1024,128]{1,0:T(8,128)(2,1)S(1)} %collective-permute-done.7.refs_6_), channel_id=1, source_target_pairs={{0,112},{16,0},{32,16},{48,32},{64,48},{80,64},{96,80},{112,96},{1... | collective-permute-start | bytes 786440 | tf_op jit(solution)/shard_map/ppermute | solution.py:275
  49.6 0.0 collective-permute-done.9
  49.6 0.3 convolution_convert_fusion.refs_7_.refs_5_.refs_3_
  49.9 9.1 %shard_map.145 = (f32[2,1,1024]{2,1,0:T(1,128)S(1)}, f32[2,1,1024]{2,1,0:T(1,128)S(1)}, f32[2,128,1024]{2,1,0:T(8,128)S(1)}) custom-call(s32[7]{0:T(128)S(1)} %pad_add_fusion.1.refs_0_, bf16[1024,128]{1,0:T(8,128)(2,1)S(1)} %constant_dynamic-update-slice_fusion.refs_1_, bf16[1024,128]{1,0:T(8,128)(2,1)S(1)} %collective-permute-done.2.refs_2_, ...), custom_call_target="tpu_custom_call" | custom-call | flops 6442450944 | bytes 1572864 | tf_op jit(solution)/shard_map/pallas_call | solution.py:220
  59.0 1.0 copy-done.2
  60.0 0.0 collective-permute-done.4.refs_2_
  60.0 0.9 broadcast_in_dim.96
  60.9 3.6 %all-to-all-start.2 = ((bf16[16,2,64,128]{3,2,1,0:T(8,128)(2,1)}), bf16[16,2,64,128]{3,2,1,0:T(8,128)(2,1)S(1)}, u32[]{:S(2)}, u32[]{:S(2)}) async-start(bf16[16,2,64,128]{3,2,1,0:T(8,128)(2,1)} %broadcast_in_dim.96), calls=%async_computation.2 | async-start | bytes 1048576 | tf_op jit(solution)/shard_map/all_to_all | solution.py:340
  64.5 0.2 select_convert_fusion.refs_5_
  64.7 1.5 %collective-permute-start.10 = (bf16[1024,128]{1,0:T(8,128)(2,1)S(1)}, bf16[1024,128]{1,0:T(8,128)(2,1)S(1)}, u32[]{:S(2)}, u32[]{:S(2)}) collective-permute-start(bf16[1024,128]{1,0:T(8,128)(2,1)S(1)} %collective-permute-done.1.refs_1_), channel_id=1, source_target_pairs={{0,16},{16,32},{32,48},{48,64},{64,80},{80,96},{96,112},{112,0},{1... | collective-permute-start | bytes 786440 | tf_op jit(solution)/shard_map/ppermute | solution.py:274
  66.2 1.2 %collective-permute-start.11 = (bf16[1024,128]{1,0:T(8,128)(2,1)S(1)}, bf16[1024,128]{1,0:T(8,128)(2,1)S(1)}, u32[]{:S(2)}, u32[]{:S(2)}) collective-permute-start(bf16[1024,128]{1,0:T(8,128)(2,1)S(1)} %collective-permute-done.4.refs_2_), channel_id=1, source_target_pairs={{0,16},{16,32},{32,48},{48,64},{64,80},{80,96},{96,112},{112,0},{1... | collective-permute-start | bytes 786440 | tf_op jit(solution)/shard_map/ppermute | solution.py:274
  67.4 1.5 %collective-permute-start.12 = (bf16[1024,128]{1,0:T(8,128)(2,1)S(1)}, bf16[1024,128]{1,0:T(8,128)(2,1)S(1)}, u32[]{:S(2)}, u32[]{:S(2)}) collective-permute-start(bf16[1024,128]{1,0:T(8,128)(2,1)S(1)} %collective-permute-done.6.refs_3_), channel_id=1, source_target_pairs={{0,112},{16,0},{32,16},{48,32},{64,48},{80,64},{96,80},{112,96},{1... | collective-permute-start | bytes 786440 | tf_op jit(solution)/shard_map/ppermute | solution.py:275
  68.9 0.2 collective-permute-start.13
  69.1 1.2 %copy-done.3 = f32[2,128,1024]{2,1,0:T(8,128)S(1)} copy-done((f32[2,128,1024]{2,1,0:T(8,128)S(1)}, f32[2,128,1024]{2,1,0:T(8,128)}, u32[]{:S(2)}) %copy-start.3) | copy-done | bytes 1048600
  70.3 5.5 %shard_map.146 = (f32[2,1,1024]{2,1,0:T(1,128)S(1)}, f32[2,1,1024]{2,1,0:T(1,128)S(1)}, f32[2,128,1024]{2,1,0:T(8,128)S(1)}) custom-call(s32[5]{0:T(128)S(1)} %get-tuple-element.69.refs_0_, bf16[1024,128]{1,0:T(8,128)(2,1)S(1)} %collective-permute-done.1.refs_1_, bf16[1024,128]{1,0:T(8,128)(2,1)S(1)} %collective-permute-done.4.refs_2_, ...), custom_call_target="tpu_custom_call" | custom-call | flops 4294967296 | bytes 1048576 | tf_op jit(solution)/shard_map/pallas_call | solution.py:220
  75.8 7.9 %collective-permute-done.10.refs_1_ = bf16[1024,128]{1,0:T(8,128)(2,1)S(1)} collective-permute-done((bf16[1024,128]{1,0:T(8,128)(2,1)S(1)}, bf16[1024,128]{1,0:T(8,128)(2,1)S(1)}, u32[]{:S(2)}, u32[]{:S(2)}) %collective-permute-start.10) | collective-permute-done | bytes 262176 | tf_op jit(solution)/shard_map/ppermute | solution.py:274
  83.7 5.6 %collective-permute-done.11.refs_2_ = bf16[1024,128]{1,0:T(8,128)(2,1)S(1)} collective-permute-done((bf16[1024,128]{1,0:T(8,128)(2,1)S(1)}, bf16[1024,128]{1,0:T(8,128)(2,1)S(1)}, u32[]{:S(2)}, u32[]{:S(2)}) %collective-permute-start.11) | collective-permute-done | bytes 262176 | tf_op jit(solution)/shard_map/ppermute | solution.py:274
  89.3 0.1 collective-permute-start.14
  89.4 2.6 %collective-permute-start.15 = (bf16[1024,128]{1,0:T(8,128)(2,1)S(1)}, bf16[1024,128]{1,0:T(8,128)(2,1)S(1)}, u32[]{:S(2)}, u32[]{:S(2)}) collective-permute-start(bf16[1024,128]{1,0:T(8,128)(2,1)S(1)} %collective-permute-done.13.refs_4_), channel_id=1, source_target_pairs={{0,112},{16,0},{32,16},{48,32},{64,48},{80,64},{96,80},{112,96},{1... | collective-permute-start | bytes 786440 | tf_op jit(solution)/shard_map/ppermute | solution.py:344
  92.0 5.4 %shard_map.147 = (f32[2,1,1024]{2,1,0:T(1,128)S(1)}, f32[2,1,1024]{2,1,0:T(1,128)S(1)}, f32[2,128,1024]{2,1,0:T(8,128)S(1)}) custom-call(s32[5]{0:T(128)S(1)} %get-tuple-element.70.refs_0_, bf16[1024,128]{1,0:T(8,128)(2,1)S(1)} %collective-permute-done.10.refs_1_, bf16[1024,128]{1,0:T(8,128)(2,1)S(1)} %collective-permute-done.11.refs_2_, ...), custom_call_target="tpu_custom_call" | custom-call | flops 4294967296 | bytes 1048576 | tf_op jit(solution)/shard_map/pallas_call | solution.py:220
  97.5 7.1 %shard_map.148 = (f32[64,2048]{1,0:T(8,128)S(1)}, bf16[64,2048]{1,0:T(8,128)(2,1)S(1)}, f32[16,128]{1,0:T(8,128)S(1)}) custom-call(s32[3]{0:T(128)S(1)} %pad_add_fusion.refs_0_, bf16[1024,128]{1,0:T(8,128)(2,1)S(1)} %collective-permute-done.14.refs_1_, bf16[1024,128]{1,0:T(8,128)(2,1)S(1)} %collective-permute-done.15.refs_2_, ...), custom_call_target="tpu_custom_call" | custom-call | flops 4294967296 | bytes 1048576 | tf_op jit(solution)/shard_map/pallas_call | solution.py:220
  104.6 0.8 copy-done
  105.4 2.6 %collective-permute-start.16 = (bf16[64,2048]{1,0:T(8,128)(2,1)S(1)}, bf16[64,2048]{1,0:T(8,128)(2,1)S(1)}, u32[]{:S(2)}, u32[]{:S(2)}) collective-permute-start(bf16[64,2048]{1,0:T(8,128)(2,1)S(1)} %get-tuple-element.63), channel_id=1, source_target_pairs={{0,8},{8,0},{1,9},{9,1},{2,10},{10,2},{3,11},{11,3},{4,12},{12,4},... | collective-permute-start | bytes 786440 | tf_op jit(solution)/shard_map/ppermute | solution.py:355
  107.9 1.2 %collective-permute-done.17.theirs_ref = f32[16,128]{1,0:T(8,128)S(1)} collective-permute-done((f32[16,128]{1,0:T(8,128)S(1)}, f32[16,128]{1,0:T(8,128)S(1)}, u32[]{:S(2)}, u32[]{:S(2)}) %collective-permute-start.17) | collective-permute-done | bytes 8224 | tf_op jit(solution)/shard_map/ppermute | solution.py:356
  109.1 0.6 copy-done.9
  109.7 0.1 copy-done.5
  109.8 2.3 %shard_map.149 = bf16[64,2048]{1,0:T(8,128)(2,1)} custom-call(f32[64,2048]{1,0:T(8,128)} %copy-done, bf16[64,2048]{1,0:T(8,128)(2,1)} %copy-done.5, f32[16,128]{1,0:T(8,128)} %copy-done.1, f32[16,128]{1,0:T(8,128)} %copy-done.9), custom_call_target="tpu_custom_call" | custom-call | tf_op jit(solution)/shard_map/pallas_call | solution.py:253
  (41 shorter events, 0.2 us)
Async XLA Ops:
  0.0 1.0 copy-start.6
  0.0 8.7 %copy-start.4 = (bf16[8,16384]{1,0:T(8,128)(2,1)S(1)}, bf16[8,16384]{1,0:T(8,128)(2,1)}, u32[]{:S(2)}) copy-start(bf16[8,16384]{1,0:T(8,128)(2,1)} %param.15) | copy-start | bytes 786436
  1.0 7.8 %copy-start.7 = (bf16[8,1024]{1,0:T(8,128)(2,1)S(1)}, bf16[8,1024]{1,0:T(8,128)(2,1)}, u32[]{:S(2)}) copy-start(bf16[8,1024]{1,0:T(8,128)(2,1)} %param.17) | copy-start | bytes 49156
  1.0 7.7 %copy-start.8 = (bf16[8,1024]{1,0:T(8,128)(2,1)S(1)}, bf16[8,1024]{1,0:T(8,128)(2,1)}, u32[]{:S(2)}) copy-start(bf16[8,1024]{1,0:T(8,128)(2,1)} %param.16) | copy-start | bytes 49156
  1.0 29.4 %collective-permute-start.2 = (bf16[1024,128]{1,0:T(8,128)(2,1)S(1)}, bf16[1024,128]{1,0:T(8,128)(2,1)S(1)}, u32[]{:S(2)}, u32[]{:S(2)}) collective-permute-start(bf16[1024,128]{1,0:T(8,128)(2,1)S(1)} %constant_dynamic-update-slice_fusion.refs_1_), channel_id=1, source_target_pairs={{0,128},{128,0},{1,129},{129,1},{2,130},{130,2},{3,131},{131,3},{4... | collective-permute-start | bytes 786440 | tf_op jit(solution)/shard_map/ppermute | solution.py:270
  3.1 41.0 %collective-permute-start = (bf16[1024,128]{1,0:T(8,128)(2,1)S(1)}, bf16[1024,128]{1,0:T(8,128)(2,1)S(1)}, u32[]{:S(2)}, u32[]{:S(2)}) collective-permute-start(bf16[1024,128]{1,0:T(8,128)(2,1)S(1)} %constant_dynamic-update-slice_fusion.refs_1_), channel_id=1, source_target_pairs={{0,16},{16,32},{32,48},{48,64},{64,80},{80,96},{96,112},{112,0},{1... | collective-permute-start | bytes 786440 | tf_op jit(solution)/shard_map/ppermute | solution.py:274
  4.8 39.9 %collective-permute-start.5 = (bf16[1024,128]{1,0:T(8,128)(2,1)S(1)}, bf16[1024,128]{1,0:T(8,128)(2,1)S(1)}, u32[]{:S(2)}, u32[]{:S(2)}) collective-permute-start(bf16[1024,128]{1,0:T(8,128)(2,1)S(1)} %constant_dynamic-update-slice_fusion.refs_1_), channel_id=1, source_target_pairs={{0,112},{16,0},{32,16},{48,32},{64,48},{80,64},{96,80},{112,96},{1... | collective-permute-start | bytes 786440 | tf_op jit(solution)/shard_map/ppermute | solution.py:275
  9.5 14.2 %all-to-all-start = ((bf16[8,8,2304]{2,0,1:T(8,128)(2,1)}), bf16[8,8,2304]{2,0,1:T(8,128)(2,1)S(1)}, u32[]{:S(2)}, u32[]{:S(2)}) async-start(bf16[8,8,2304]{2,0,1:T(8,128)(2,1)} %pad_maximum_fusion), calls=%async_computation | async-start | bytes 589824 | tf_op jit(solution)/shard_map/all_to_all | solution.py:291
  16.5 0.7 copy-start.15
  17.3 0.7 copy-start.13
  17.3 0.7 copy-start.14
  18.0 0.7 copy-start.10
  18.0 0.7 copy-start.11
  18.0 0.7 copy-start.12
  24.7 13.3 %all-to-all-start.1 = ((bf16[16,4,2048]{2,1,0:T(4,128)(2,1)}), bf16[16,4,2048]{2,1,0:T(4,128)(2,1)S(1)}, u32[]{:S(2)}, u32[]{:S(2)}) async-start(bf16[16,4,2048]{2,1,0:T(4,128)(2,1)} %all_to_all.26), calls=%async_computation.1 | async-start | bytes 524288 | tf_op jit(solution)/shard_map/all_to_all | solution.py:300
  30.5 16.4 %collective-permute-start.3 = (bf16[1024,128]{1,0:T(8,128)(2,1)S(1)}, bf16[1024,128]{1,0:T(8,128)(2,1)S(1)}, u32[]{:S(2)}, u32[]{:S(2)}) collective-permute-start(bf16[1024,128]{1,0:T(8,128)(2,1)S(1)} %collective-permute-done.2.refs_2_), channel_id=1, source_target_pairs={{0,16},{16,32},{32,48},{48,64},{64,80},{80,96},{96,112},{112,0},{1... | collective-permute-start | bytes 786440 | tf_op jit(solution)/shard_map/ppermute | solution.py:274
  31.9 15.0 %collective-permute-start.7 = (bf16[1024,128]{1,0:T(8,128)(2,1)S(1)}, bf16[1024,128]{1,0:T(8,128)(2,1)S(1)}, u32[]{:S(2)}, u32[]{:S(2)}) collective-permute-start(bf16[1024,128]{1,0:T(8,128)(2,1)S(1)} %collective-permute-done.2.refs_2_), channel_id=1, source_target_pairs={{0,112},{16,0},{32,16},{48,32},{64,48},{80,64},{96,80},{112,96},{1... | collective-permute-start | bytes 786440 | tf_op jit(solution)/shard_map/ppermute | solution.py:275
  38.1 11.5 %collective-permute-start.9 = (bf16[64,2048]{1,0:T(8,128)(2,1)S(1)}, bf16[64,2048]{1,0:T(8,128)(2,1)S(1)}, u32[]{:S(2)}, u32[]{:S(2)}) collective-permute-start(bf16[64,2048]{1,0:T(8,128)(2,1)S(1)} %all_to_all.28), channel_id=1, source_target_pairs={{0,8},{8,0},{1,9},{9,1},{2,10},{10,2},{3,11},{11,3},{4,12},{12,4},... | collective-permute-start | bytes 786440 | tf_op jit(solution)/shard_map/ppermute | solution.py:301
  44.1 15.9 %collective-permute-start.1 = (bf16[1024,128]{1,0:T(8,128)(2,1)S(1)}, bf16[1024,128]{1,0:T(8,128)(2,1)S(1)}, u32[]{:S(2)}, u32[]{:S(2)}) collective-permute-start(bf16[1024,128]{1,0:T(8,128)(2,1)S(1)} %collective-permute-done.refs_3_), channel_id=1, source_target_pairs={{0,16},{16,32},{32,48},{48,64},{64,80},{80,96},{96,112},{112,0},{1... | collective-permute-start | bytes 786440 | tf_op jit(solution)/shard_map/ppermute | solution.py:274
  44.7 15.3 %collective-permute-start.6 = (bf16[1024,128]{1,0:T(8,128)(2,1)S(1)}, bf16[1024,128]{1,0:T(8,128)(2,1)S(1)}, u32[]{:S(2)}, u32[]{:S(2)}) collective-permute-start(bf16[1024,128]{1,0:T(8,128)(2,1)S(1)} %collective-permute-done.5.refs_5_), channel_id=1, source_target_pairs={{0,112},{16,0},{32,16},{48,32},{64,48},{80,64},{96,80},{112,96},{1... | collective-permute-start | bytes 786440 | tf_op jit(solution)/shard_map/ppermute | solution.py:275
  46.9 13.1 %collective-permute-start.4 = (bf16[1024,128]{1,0:T(8,128)(2,1)S(1)}, bf16[1024,128]{1,0:T(8,128)(2,1)S(1)}, u32[]{:S(2)}, u32[]{:S(2)}) collective-permute-start(bf16[1024,128]{1,0:T(8,128)(2,1)S(1)} %collective-permute-done.3.refs_4_), channel_id=1, source_target_pairs={{0,16},{16,32},{32,48},{48,64},{64,80},{80,96},{96,112},{112,0},{1... | collective-permute-start | bytes 786440 | tf_op jit(solution)/shard_map/ppermute | solution.py:274
  46.9 13.1 %collective-permute-start.8 = (bf16[1024,128]{1,0:T(8,128)(2,1)S(1)}, bf16[1024,128]{1,0:T(8,128)(2,1)S(1)}, u32[]{:S(2)}, u32[]{:S(2)}) collective-permute-start(bf16[1024,128]{1,0:T(8,128)(2,1)S(1)} %collective-permute-done.7.refs_6_), channel_id=1, source_target_pairs={{0,112},{16,0},{32,16},{48,32},{64,48},{80,64},{96,80},{112,96},{1... | collective-permute-start | bytes 786440 | tf_op jit(solution)/shard_map/ppermute | solution.py:275
  59.0 1.0 copy-start.2
  60.9 36.6 %all-to-all-start.2 = ((bf16[16,2,64,128]{3,2,1,0:T(8,128)(2,1)}), bf16[16,2,64,128]{3,2,1,0:T(8,128)(2,1)S(1)}, u32[]{:S(2)}, u32[]{:S(2)}) async-start(bf16[16,2,64,128]{3,2,1,0:T(8,128)(2,1)} %broadcast_in_dim.96), calls=%async_computation.2 | async-start | bytes 1048576 | tf_op jit(solution)/shard_map/all_to_all | solution.py:340
  64.7 19.0 %collective-permute-start.10 = (bf16[1024,128]{1,0:T(8,128)(2,1)S(1)}, bf16[1024,128]{1,0:T(8,128)(2,1)S(1)}, u32[]{:S(2)}, u32[]{:S(2)}) collective-permute-start(bf16[1024,128]{1,0:T(8,128)(2,1)S(1)} %collective-permute-done.1.refs_1_), channel_id=1, source_target_pairs={{0,16},{16,32},{32,48},{48,64},{64,80},{80,96},{96,112},{112,0},{1... | collective-permute-start | bytes 786440 | tf_op jit(solution)/shard_map/ppermute | solution.py:274
  66.2 23.1 %collective-permute-start.11 = (bf16[1024,128]{1,0:T(8,128)(2,1)S(1)}, bf16[1024,128]{1,0:T(8,128)(2,1)S(1)}, u32[]{:S(2)}, u32[]{:S(2)}) collective-permute-start(bf16[1024,128]{1,0:T(8,128)(2,1)S(1)} %collective-permute-done.4.refs_2_), channel_id=1, source_target_pairs={{0,16},{16,32},{32,48},{48,64},{64,80},{80,96},{96,112},{112,0},{1... | collective-permute-start | bytes 786440 | tf_op jit(solution)/shard_map/ppermute | solution.py:274
  67.4 21.9 %collective-permute-start.12 = (bf16[1024,128]{1,0:T(8,128)(2,1)S(1)}, bf16[1024,128]{1,0:T(8,128)(2,1)S(1)}, u32[]{:S(2)}, u32[]{:S(2)}) collective-permute-start(bf16[1024,128]{1,0:T(8,128)(2,1)S(1)} %collective-permute-done.6.refs_3_), channel_id=1, source_target_pairs={{0,112},{16,0},{32,16},{48,32},{64,48},{80,64},{96,80},{112,96},{1... | collective-permute-start | bytes 786440 | tf_op jit(solution)/shard_map/ppermute | solution.py:275
  68.9 20.4 %collective-permute-start.13 = (bf16[1024,128]{1,0:T(8,128)(2,1)S(1)}, bf16[1024,128]{1,0:T(8,128)(2,1)S(1)}, u32[]{:S(2)}, u32[]{:S(2)}) collective-permute-start(bf16[1024,128]{1,0:T(8,128)(2,1)S(1)} %collective-permute-done.8.refs_4_), channel_id=1, source_target_pairs={{0,112},{16,0},{32,16},{48,32},{64,48},{80,64},{96,80},{112,96},{1... | collective-permute-start | bytes 786440 | tf_op jit(solution)/shard_map/ppermute | solution.py:275
  69.1 1.2 %copy-start.3 = (f32[2,128,1024]{2,1,0:T(8,128)S(1)}, f32[2,128,1024]{2,1,0:T(8,128)}, u32[]{:S(2)}) copy-start(f32[2,128,1024]{2,1,0:T(8,128)} %copy-done.2) | copy-start | bytes 3145732
  89.3 8.1 %collective-permute-start.14 = (bf16[1024,128]{1,0:T(8,128)(2,1)S(1)}, bf16[1024,128]{1,0:T(8,128)(2,1)S(1)}, u32[]{:S(2)}, u32[]{:S(2)}) collective-permute-start(bf16[1024,128]{1,0:T(8,128)(2,1)S(1)} %collective-permute-done.10.refs_1_), channel_id=1, source_target_pairs={{0,16},{16,32},{32,48},{48,64},{64,80},{80,96},{96,112},{112,0},{1... | collective-permute-start | bytes 786440 | tf_op jit(solution)/shard_map/ppermute | solution.py:343
  89.4 8.1 %collective-permute-start.15 = (bf16[1024,128]{1,0:T(8,128)(2,1)S(1)}, bf16[1024,128]{1,0:T(8,128)(2,1)S(1)}, u32[]{:S(2)}, u32[]{:S(2)}) collective-permute-start(bf16[1024,128]{1,0:T(8,128)(2,1)S(1)} %collective-permute-done.13.refs_4_), channel_id=1, source_target_pairs={{0,112},{16,0},{32,16},{48,32},{64,48},{80,64},{96,80},{112,96},{1... | collective-permute-start | bytes 786440 | tf_op jit(solution)/shard_map/ppermute | solution.py:344
  104.6 0.8 copy-start
  105.4 3.7 %copy-start.1 = (f32[16,128]{1,0:T(8,128)}, f32[16,128]{1,0:T(8,128)S(1)}, u32[]{:S(2)}) copy-start(f32[16,128]{1,0:T(8,128)S(1)} %get-tuple-element.64.mine_ref) | copy-start | bytes 24580
  105.4 3.7 %collective-permute-start.16 = (bf16[64,2048]{1,0:T(8,128)(2,1)S(1)}, bf16[64,2048]{1,0:T(8,128)(2,1)S(1)}, u32[]{:S(2)}, u32[]{:S(2)}) collective-permute-start(bf16[64,2048]{1,0:T(8,128)(2,1)S(1)} %get-tuple-element.63), channel_id=1, source_target_pairs={{0,8},{8,0},{1,9},{9,1},{2,10},{10,2},{3,11},{11,3},{4,12},{12,4},... | collective-permute-start | bytes 786440 | tf_op jit(solution)/shard_map/ppermute | solution.py:355
  107.9 1.2 %collective-permute-start.17 = (f32[16,128]{1,0:T(8,128)S(1)}, f32[16,128]{1,0:T(8,128)S(1)}, u32[]{:S(2)}, u32[]{:S(2)}) collective-permute-start(f32[16,128]{1,0:T(8,128)S(1)} %get-tuple-element.64.mine_ref), channel_id=1, source_target_pairs={{0,8},{8,0},{1,9},{9,1},{2,10},{10,2},{3,11},{11,3},{4,12},{12,4},... | collective-permute-start | bytes 24584 | tf_op jit(solution)/shard_map/ppermute | solution.py:356
  109.1 0.6 copy-start.9
  109.1 0.7 copy-start.5
where the time goes:
time: 113 us; the launch traced here: 112 us
  starting transfers between devices  47 us (42%)
  Pallas kernels  29.4 us (26%)
  waiting for transfers between devices  24.2 us (21%)
  local copies, waits for them, and re-layouts  8.53 us (8%)
  other arithmetic  1.53 us (1%)
    pallas_call x4, Pallas kernels, attend(): pl.pallas_call(functools.partial(attend_kernel, n_cached, fresh is not No...  27.1 us
    ppermute x3, waiting for transfers between devices, hop(): lax.ppermute(above[0], 'z', up)  7.9 us
    ppermute x3, starting transfers between devices, hop(): lax.ppermute(below[0], 'z', down)  7.59 us
    unnamed x33, local copies, waits for them, and re-layouts  6.63 us
    all_to_all x1, starting transfers between devices, step(): mixed = lax.all_to_all(mixed, 'tp', split_axis=1, concat_axis=0, tiled=True)  6.36 us
    ppermute x1, starting transfers between devices, step(): peers = lax.ppermute(mine, 'c', swap)  6.03 us
    ppermute x3, waiting for transfers between devices, hop(): lax.ppermute(above[1], 'z', up)  5.62 us
    all_to_all x1, starting transfers between devices, step(): lax.all_to_all(arranged, ('x', 'z'), split_axis=0, concat_axis=0, tiled=T...  5.54 us
  transfers between devices with their start and end apart: 21, of which 5 were waited for; matrix products, arithmetic and copies ran while one was open for 2% of the time, Pallas kernels for 18%

commit v1 on v0

--- a/solution.py
+++ b/solution.py
@@ -19,11 +19,12 @@
 f32 = jnp.float32
 
 
-def attend_kernel(n_cached, has_fresh, first, last, rows, heads, *refs):
+def attend_kernel(places, n_arrays, has_fresh, first, last, rows, heads, *refs):
     info = refs[0]
     at = 1
-    cached = refs[at : at + n_cached]
-    at += n_cached
+    n_cached = len(places)
+    arrays = refs[at : at + n_arrays]
+    at += n_arrays
     q_ref = refs[at]
     at += 1
     if has_fresh:
@@ -48,11 +49,12 @@
 
     def copies(i, slot):
         row = pl.multiple_of(slot * BLOCK, BLOCK)
+        source, top = arrays[places[i][0]], places[i][1]
         return (
             pltpu.make_async_copy(
-                cached[i].at[pl.ds(0, BLOCK), :], kbuf.at[pl.ds(row, BLOCK), pl.ds(0, HEAD_SIZE)], sems.at[i]
+                source.at[pl.ds(top, BLOCK), :], kbuf.at[pl.ds(row, BLOCK), pl.ds(0, HEAD_SIZE)], sems.at[i]
             ),
-            pltpu.make_async_copy(cached[i].at[pl.ds(BLOCK, BLOCK), :], vbuf.at[pl.ds(row, BLOCK), :], sems.at[i]),
+            pltpu.make_async_copy(source.at[pl.ds(top + BLOCK, BLOCK), :], vbuf.at[pl.ds(row, BLOCK), :], sems.at[i]),
         )
 
     def visit(action):
@@ -78,7 +80,10 @@
         lax.broadcasted_iota(jnp.int32, (rows, HEAD_SIZE), 0) == lax.broadcasted_iota(jnp.int32, (rows, HEAD_SIZE), 1)
     ).astype(bf16)
     for h in range(heads):
-        qbuf[pl.ds(h * rows, rows), 0:HEAD_SIZE] = q_ref[:, h * HEAD_SIZE : (h + 1) * HEAD_SIZE]
+        side, col = divmod(h, heads // 2)
+        qbuf[pl.ds(h * rows, rows), 0:HEAD_SIZE] = q_ref[
+            side * rows : (side + 1) * rows, col * HEAD_SIZE : (col + 1) * HEAD_SIZE
+        ]
         qbuf[pl.ds(h * rows, rows), HEAD_SIZE : 2 * HEAD_SIZE] = eye
 
     def bias(i, slot):
@@ -176,16 +181,16 @@
                 lse_ref[h : h + 1, :] = lse[:, j * rows : (j + 1) * rows]
 
 
-def attend(info, cached, queries, heads, fresh=None, state=None, last=False):
-    rows = queries.shape[0]
+def attend(info, arrays, places, queries, heads, fresh=None, state=None, last=False):
+    rows = queries.shape[0] // 2
     wide = GROUP * rows
     groups = heads // GROUP
     first = state is None
-    n_cached = len(cached)
+    n_cached = len(places)
     slots = n_cached + (0 if fresh is None else fresh[0].shape[0] * fresh[0].shape[2] // BLOCK)
     vm = pl.BlockSpec(memory_space=pltpu.VMEM)
-    args = [info, *cached, queries]
-    specs = [pl.BlockSpec(memory_space=pltpu.SMEM)] + [pl.BlockSpec(memory_space=pl.ANY)] * n_cached + [vm]
+    args = [info, *arrays, queries]
+    specs = [pl.BlockSpec(memory_space=pltpu.SMEM)] + [pl.BlockSpec(memory_space=pl.ANY)] * len(arrays) + [vm]
     if fresh is not None:
         args += list(fresh)
         specs += [vm, vm]
@@ -218,12 +223,12 @@
     if last:
         scratch += [pltpu.VMEM(s, d) for s, d in states]
     return pl.pallas_call(
-        functools.partial(attend_kernel, n_cached, fresh is not None, first, last, rows, heads),
+        functools.partial(attend_kernel, places, len(arrays), fresh is not None, first, last, rows, heads),
         out_shape=outs,
         in_specs=specs,
         out_specs=[vm] * 3,
         scratch_shapes=scratch,
-        compiler_params=pltpu.CompilerParams(vmem_limit_bytes=40 * 2**20),
+        compiler_params=pltpu.CompilerParams(vmem_limit_bytes=24 * 2**20),
         cost_estimate=pl.CostEstimate(
             flops=4 * slots * BLOCK * heads * rows * HEAD_SIZE * 2,
             bytes_accessed=slots * BLOCK * HEAD_SIZE * 4,
@@ -255,6 +260,7 @@
         out_shape=jax.ShapeDtypeStruct(keep.shape, bf16),
         in_specs=[pl.BlockSpec(memory_space=pltpu.VMEM)] * 4,
         out_specs=pl.BlockSpec(memory_space=pltpu.VMEM),
+        compiler_params=pltpu.CompilerParams(vmem_limit_bytes=8 * 2**20),
     )(keep, got, mine, theirs)
 
 
@@ -269,13 +275,12 @@
     own = jnp.concatenate([cached_key_rows, cached_value_rows], axis=0)
     other = lax.ppermute(own, "x", swap)
 
+    both = jnp.concatenate([own, other], axis=0)
+
     def hop(above, below):
-        return (
-            (lax.ppermute(above[0], "z", up), lax.ppermute(above[1], "z", up)),
-            (lax.ppermute(below[0], "z", down), lax.ppermute(below[1], "z", down)),
-        )
-
-    up1, down1 = hop((own, other), (own, other))
+        return lax.ppermute(above, "z", up), lax.ppermute(below, "z", down)
+
+    up1, down1 = hop(both, both)
     up2, down2 = hop(up1, down1)
 
     local = query.shape[0]
@@ -294,20 +299,36 @@
     heads = width // HEAD_SIZE
     order = jnp.arange(parts, dtype=jnp.int32)
     inverse = jnp.sum(jnp.where(stripe_owner[None, :] == order[:, None], order[None, :], 0), axis=1)
-    row_of = (inverse[:, None] * stripe + jnp.arange(stripe, dtype=jnp.int32)[None, :]).reshape(rows)
-    pick = (row_of[:, None] == jnp.arange(rows, dtype=jnp.int32)[None, :]).astype(bf16)
-    arranged = jnp.dot(pick, mixed[:, :width], preferred_element_type=f32).astype(bf16)
+    half = width // 2
+    chips = nx * nz
+    per = rows // chips
+    out_id = jnp.arange(2 * rows, dtype=jnp.int32)
+    wanted = out_id // (2 * per) * per + out_id % per
+    side = out_id // per % 2
+    from_row = jnp.sum(jnp.where((wanted // stripe)[:, None] == order[None, :], inverse[None, :], 0), axis=1)
+    from_row = from_row * stripe + wanted % stripe
+    pick = (from_row[:, None] == jnp.arange(rows, dtype=jnp.int32)[None, :])
+    left = (pick & (side == 0)[:, None]).astype(bf16)
+    right = (pick & (side == 1)[:, None]).astype(bf16)
+    arranged = jnp.dot(
+        jnp.concatenate([left, right], axis=1),
+        jnp.concatenate([mixed[:, :half], mixed[:, half:width]], axis=0),
+        preferred_element_type=f32,
+    ).astype(bf16)
     mine = lax.all_to_all(arranged, ("x", "z"), split_axis=0, concat_axis=0, tiled=True)
     peers = lax.ppermute(mine, "c", swap)
 
-    def spot(rel, s, src, i):
+    def spot(side, rel, s, src, i):
         part = (src != c).astype(jnp.int32)
         owner = jnp.where(rel == 0, c, 1 - c)
-        return part * rows + (s * nc + owner) * stripe + i
+        return part * 2 * rows + s * 2 * per + side * per + owner * stripe + i
 
     idx = jnp.arange(nc * rows, dtype=jnp.int32)
-    i_, src_, s_, rel_ = idx % stripe, idx // stripe % nc, idx // (stripe * nc) % (nx * nz), idx // rows
-    choose = (spot(rel_, s_, src_, i_)[:, None] == idx[None, :]).astype(bf16)
+    i_, src_, s_, rel_ = idx % stripe, idx // stripe % nc, idx // (stripe * nc) % chips, idx // rows
+    wide_id = jnp.arange(2 * nc * rows, dtype=jnp.int32)
+    low = wide_id % (nc * rows)
+    where = spot(wide_id // (nc * rows), low // rows, low // (stripe * nc) % chips, low // stripe % nc, low % stripe)
+    choose = (where[:, None] == wide_id[None, :]).astype(bf16)
     queries = jnp.dot(choose, jnp.concatenate([mine, peers], axis=0), preferred_element_type=f32).astype(bf16)
     owner_ = (x * nz + z) * nc + jnp.where(rel_ == 0, c, 1 - c)
     residue_ = jnp.sum(jnp.where(owner_[:, None] == order[None, :], inverse[None, :], 0), axis=1)
@@ -331,21 +352,24 @@
     def around(step):
         return [(0, -step), (1, -step), (0, step), (1, step)]
 
+    two = 2 * slots
+    near = ((0, 0), (0, two), (1, 0), (1, two), (2, 0), (2, two))
+    pair = ((0, 0), (0, two), (1, 0), (1, two))
     first_info = info_of([(0, 0), (1, 0)] + around(1))
-    state = attend(first_info, [own, other, *up1, *down1], queries, heads)
+    state = attend(first_info, [both, up1, down1], near, queries, heads)
     up2, down2, state = lax.optimization_barrier((up2, down2, state))
     up3, down3 = hop(up2, down2)
-    fresh, state = lax.optimization_barrier((fresh, state))
-    fresh = jnp.broadcast_to(fresh, (nx * nz, 2, rows, HEAD_SIZE))
+    state = attend(info_of(around(2)), [up2, down2], pair, queries, heads, state=state)
+    up3, down3, fresh, state = lax.optimization_barrier((up3, down3, fresh, state))
+    up4 = lax.ppermute(up3[:two], "z", up)
+    down4 = lax.ppermute(down3[two:], "z", down)
+    fresh = jnp.broadcast_to(fresh, (chips, 2, rows, HEAD_SIZE))
     fresh = lax.all_to_all(fresh, ("x", "z"), split_axis=0, concat_axis=0, tiled=True)
-    state = attend(info_of(around(2)), [*up2, *down2], queries, heads, state=state)
-    up3, down3, state = lax.optimization_barrier((up3, down3, state))
-    far_own = lax.ppermute(up3[0], "z", up)
-    far_other = lax.ppermute(down3[1], "z", down)
-    state = attend(info_of(around(3)), [*up3, *down3], queries, heads, state=state)
+    state = attend(info_of(around(3)), [up3, down3], pair, queries, heads, state=state)
     keep, give, lse = attend(
         info_of([(0, 4), (1, 4)]),
-        [far_own, far_other],
+        [up4, down4],
+        ((0, 0), (1, 0)),
         queries,
         heads,
         fresh=(fresh, fresh_mask),

time: 113 us -> 109 us (0.965)
  local copies, waits for them, and re-layouts: 8.53 us -> 5.53 us
  starting transfers between devices: 47 us -> 44.2 us
    ppermute x14 -> x8, starting transfers between devices: 20.8 us -> 11 us  [the longest x6 8.19 us: hop(): return (lax.ppermute(above, 'z', up), lax.ppermute(below, 'z', down))]
    all_to_all x1, starting transfers between devices: 3.57 us -> 7.9 us  [step(): lax.all_to_all(fresh, ('x', 'z'), split_axis=0, concat_axis=0, tiled=True)]
    all_to_all x1, starting transfers between devices: 5.54 us -> 8.32 us  [step(): lax.all_to_all(arranged, ('x', 'z'), split_axis=0, concat_axis=0, tiled=T...]
    unnamed x33 -> x26, local copies, waits for them, and re-layouts: 6.63 us -> 4.52 us
    ppermute x1, starting transfers between devices: 2.12 us -> 0.4 us  [step(): other = lax.ppermute(own, 'x', swap)]
    all_to_all x1, starting transfers between devices: 6.36 us -> 7.6 us  [step(): mixed = lax.all_to_all(mixed, 'tp', split_axis=1, concat_axis=0, tiled=True)]
    ppermute x14 -> x8, waiting for transfers between devices: 13.5 us -> 13.4 us  [the longest x1 9.38 us: step(): up4 = lax.ppermute(up3[:two], 'z', up)]
  transfers between devices with their start and end apart: 21 -> 15, of which waited for: 5 -> 5; matrix products, arithmetic and copies ran while one was open for 2% -> 2% of each run, Pallas kernels for 18% -> 19%
where the time goes in v1:
time: 109 us; the launch traced here: 107 us
  starting transfers between devices  44.2 us (41%)
  Pallas kernels  28.3 us (26%)
  waiting for transfers between devices  24.5 us (22%)
  local copies, waits for them, and re-layouts  5.53 us (5%)
  other arithmetic  2.6 us (2%)
  matrix products  1.32 us (1%)
    pallas_call x4, Pallas kernels, attend(): pl.pallas_call(functools.partial(attend_kernel, places, len(arrays), fres...  27.2 us
    ppermute x1, waiting for transfers between devices, step(): up4 = lax.ppermute(up3[:two], 'z', up)  9.38 us
    all_to_all x1, starting transfers between devices, step(): lax.all_to_all(arranged, ('x', 'z'), split_axis=0, concat_axis=0, tiled=T...  8.32 us
    ppermute x6, starting transfers between devices, hop(): return (lax.ppermute(above, 'z', up), lax.ppermute(below, 'z', down))  8.19 us
    all_to_all x1, starting transfers between devices, step(): lax.all_to_all(fresh, ('x', 'z'), split_axis=0, concat_axis=0, tiled=True)  7.9 us
    all_to_all x1, starting transfers between devices, step(): mixed = lax.all_to_all(mixed, 'tp', split_axis=1, concat_axis=0, tiled=True)  7.6 us
    ppermute x1, starting transfers between devices, step(): peers = lax.ppermute(mine, 'c', swap)  6.47 us
    all_to_all x1, waiting for transfers between devices, step(): mixed = lax.all_to_all(mixed, 'tp', split_axis=1, concat_axis=0, tiled=True)  5.78 us
  transfers between devices with their start and end apart: 15, of which 5 were waited for; matrix products, arithmetic and copies ran while one was open for 2% of the time, Pallas kernels for 19%

profile of v1, /device:TPU:1, one launch (start us, length us, event | category | flops | bytes accessed | tf_op | source)
XLA Modules:
  0.0 107.4 jit_solution(11947599948839198899)
XLA Ops:
  0.0 1.7 %pad_maximum_fusion = bf16[8,8,2304]{2,0,1:T(8,128)(2,1)} fusion(bf16[8,8,128]{2,0,1:T(8,128)(2,1)} %bitcast.17, bf16[8,8,128]{2,0,1:T(8,128)(2,1)} %bitcast.18, bf16[8,8,2048]{2,0,1:T(8,128)(2,1)} %bitcast.13), kind=kLoop, calls=%fused_computation.7 | loop fusion | flops 884736 | bytes 589824 | tf_op jit(solution)/shard_map/concatenate | solution.py:288
  1.7 7.6 %all-to-all-start = ((bf16[8,8,2304]{2,0,1:T(8,128)(2,1)}), bf16[8,8,2304]{2,0,1:T(8,128)(2,1)S(1)}, u32[]{:S(2)}, u32[]{:S(2)}) async-start(bf16[8,8,2304]{2,0,1:T(8,128)(2,1)} %pad_maximum_fusion), calls=%async_computation | async-start | bytes 589824 | tf_op jit(solution)/shard_map/all_to_all | solution.py:296
  9.3 0.0 copy-done.4
  9.3 0.0 copy-done.5
  9.4 0.4 collective-permute-start
  9.8 0.0 copy-start.11
  9.8 0.6 copy-done.11
  10.4 0.1 select_reduce_fusion.2
  10.6 0.1 select_reduce_fusion
  10.7 0.0 copy-start.10
  10.7 0.6 copy-done.8
  11.3 0.0 copy-done.9
  11.3 0.0 copy-done.10
  11.4 0.1 fusion.9
  11.5 5.8 %all-to-all-done = bf16[8,8,2304]{2,0,1:T(8,128)(2,1)S(1)} async-done(((bf16[8,8,2304]{2,0,1:T(8,128)(2,1)}), bf16[8,8,2304]{2,0,1:T(8,128)(2,1)S(1)}, u32[]{:S(2)}, u32[]{:S(2)}) %all-to-all-start) | async-done | bytes 294944 | tf_op jit(solution)/shard_map/all_to_all | solution.py:296
  17.3 1.0 fusion
  18.3 8.3 %all-to-all-start.1 = ((bf16[16,8,1024]{2,1,0:T(8,128)(2,1)}), bf16[16,8,1024]{2,1,0:T(8,128)(2,1)S(1)}, u32[]{:S(2)}, u32[]{:S(2)}) async-start(bf16[16,8,1024]{2,1,0:T(8,128)(2,1)} %fusion), calls=%async_computation.1 | async-start | bytes 524288 | tf_op jit(solution)/shard_map/all_to_all | solution.py:318
  27.3 0.0 copy-start.6
  27.3 0.0 copy-start.7
  27.3 0.0 collective-permute-done
  27.4 1.4 %collective-permute-start.1 = (bf16[2048,128]{1,0:T(8,128)(2,1)S(1)}, bf16[2048,128]{1,0:T(8,128)(2,1)S(1)}, u32[]{:S(2)}, u32[]{:S(2)}) collective-permute-start(bf16[2048,128]{1,0:T(8,128)(2,1)S(1)} %constant_dynamic-update-slice_fusion.refs_1_), channel_id=1, source_target_pairs={{0,16},{16,32},{32,48},{48,64},{64,80},{80,96},{96,112},{112,0},{1... | collective-permute-start | bytes 1572872 | tf_op jit(solution)/shard_map/ppermute | solution.py:281
  28.8 1.3 %collective-permute-start.3 = (bf16[2048,128]{1,0:T(8,128)(2,1)S(1)}, bf16[2048,128]{1,0:T(8,128)(2,1)S(1)}, u32[]{:S(2)}, u32[]{:S(2)}) collective-permute-start(bf16[2048,128]{1,0:T(8,128)(2,1)S(1)} %constant_dynamic-update-slice_fusion.refs_1_), channel_id=1, source_target_pairs={{0,112},{16,0},{32,16},{48,32},{64,48},{80,64},{96,80},{112,96},{1... | collective-permute-start | bytes 1572872 | tf_op jit(solution)/shard_map/ppermute | solution.py:281
  30.2 0.0 copy-done.6
  30.2 0.0 copy-done.7
  30.2 4.2 %all-to-all-done.1 = bf16[16,8,1024]{2,1,0:T(8,128)(2,1)S(1)} async-done(((bf16[16,8,1024]{2,1,0:T(8,128)(2,1)}), bf16[16,8,1024]{2,1,0:T(8,128)(2,1)S(1)}, u32[]{:S(2)}, u32[]{:S(2)}) %all-to-all-start.1) | async-done | bytes 262176 | tf_op jit(solution)/shard_map/all_to_all | solution.py:318
  34.4 6.5 %collective-permute-start.5 = (bf16[128,1024]{1,0:T(8,128)(2,1)S(1)}, bf16[128,1024]{1,0:T(8,128)(2,1)S(1)}, u32[]{:S(2)}, u32[]{:S(2)}) collective-permute-start(bf16[128,1024]{1,0:T(8,128)(2,1)S(1)} %bitcast.14), channel_id=1, source_target_pairs={{0,8},{8,0},{1,9},{9,1},{2,10},{10,2},{3,11},{11,3},{4,12},{12,4},... | collective-permute-start | bytes 786440 | tf_op jit(solution)/shard_map/ppermute | solution.py:319
  40.9 0.1 pad_add_fusion.1.refs_0_
  41.0 0.1 pad_add_fusion.2
  41.0 4.0 %collective-permute-done.1.refs_2_ = bf16[2048,128]{1,0:T(8,128)(2,1)S(1)} collective-permute-done((bf16[2048,128]{1,0:T(8,128)(2,1)S(1)}, bf16[2048,128]{1,0:T(8,128)(2,1)S(1)}, u32[]{:S(2)}, u32[]{:S(2)}) %collective-permute-start.1) | collective-permute-done | bytes 524320 | tf_op jit(solution)/shard_map/ppermute | solution.py:281
  45.0 0.0 collective-permute-start.2
  45.0 0.0 collective-permute-done.3.refs_3_
  45.0 2.7 %collective-permute-start.4 = (bf16[2048,128]{1,0:T(8,128)(2,1)S(1)}, bf16[2048,128]{1,0:T(8,128)(2,1)S(1)}, u32[]{:S(2)}, u32[]{:S(2)}) collective-permute-start(bf16[2048,128]{1,0:T(8,128)(2,1)S(1)} %collective-permute-done.3.refs_3_), channel_id=1, source_target_pairs={{0,112},{16,0},{32,16},{48,32},{64,48},{80,64},{96,80},{112,96},{1... | collective-permute-start | bytes 1572872 | tf_op jit(solution)/shard_map/ppermute | solution.py:281
  47.7 0.0 collective-permute-done.5
  47.7 0.3 convolution_convert_fusion.refs_4_.refs_3_
  48.0 9.1 %shard_map.145 = (f32[2,1,1024]{2,1,0:T(1,128)S(1)}, f32[2,1,1024]{2,1,0:T(1,128)S(1)}, f32[2,128,1024]{2,1,0:T(8,128)S(1)}) custom-call(s32[7]{0:T(128)S(1)} %pad_add_fusion.1.refs_0_, bf16[2048,128]{1,0:T(8,128)(2,1)S(1)} %constant_dynamic-update-slice_fusion.refs_1_, bf16[2048,128]{1,0:T(8,128)(2,1)S(1)} %collective-permute-done.1.refs_2_, ...), custom_call_target="tpu_custom_call" | custom-call | flops 6442450944 | bytes 1572864 | tf_op jit(solution)/shard_map/pallas_call | solution.py:225
  57.1 0.0 collective-permute-done.2.refs_1_
  57.1 0.0 collective-permute-done.4.refs_2_
  57.1 0.5 collective-permute-start.6
  57.7 2.2 %collective-permute-start.7 = (bf16[2048,128]{1,0:T(8,128)(2,1)S(1)}, bf16[2048,128]{1,0:T(8,128)(2,1)S(1)}, u32[]{:S(2)}, u32[]{:S(2)}) collective-permute-start(bf16[2048,128]{1,0:T(8,128)(2,1)S(1)} %collective-permute-done.4.refs_2_), channel_id=1, source_target_pairs={{0,112},{16,0},{32,16},{48,32},{64,48},{80,64},{96,80},{112,96},{1... | collective-permute-start | bytes 1572872 | tf_op jit(solution)/shard_map/ppermute | solution.py:281
  59.9 5.6 %shard_map.146 = (f32[2,1,1024]{2,1,0:T(1,128)S(1)}, f32[2,1,1024]{2,1,0:T(1,128)S(1)}, f32[2,128,1024]{2,1,0:T(8,128)S(1)}) custom-call(s32[5]{0:T(128)S(1)} %get-tuple-element.61.refs_0_, bf16[2048,128]{1,0:T(8,128)(2,1)S(1)} %collective-permute-done.2.refs_1_, bf16[2048,128]{1,0:T(8,128)(2,1)S(1)} %collective-permute-done.4.refs_2_, ...), custom_call_target="tpu_custom_call" | custom-call | flops 4294967296 | bytes 1048576 | tf_op jit(solution)/shard_map/pallas_call | solution.py:225
  65.5 0.0 copy-start.2
  65.5 1.0 copy-done.2
  66.5 0.0 collective-permute-done.6.refs_1_
  66.5 0.0 collective-permute-done.7.refs_2_
  66.5 0.9 broadcast_in_dim.112
  67.4 7.9 %all-to-all-start.2 = ((bf16[16,2,64,128]{3,2,1,0:T(8,128)(2,1)}), bf16[16,2,64,128]{3,2,1,0:T(8,128)(2,1)S(1)}, u32[]{:S(2)}, u32[]{:S(2)}) async-start(bf16[16,2,64,128]{3,2,1,0:T(8,128)(2,1)} %broadcast_in_dim.112), calls=%async_computation.2 | async-start | bytes 1048576 | tf_op jit(solution)/shard_map/all_to_all | solution.py:367
  75.4 0.0 copy-start.3
  75.4 0.1 pad_add_fusion.refs_0_
  75.5 0.2 select_convert_fusion.refs_5_
  75.7 1.4 %collective-permute-start.8 = (bf16[1024,128]{1,0:T(8,128)(2,1)S(1)}, bf16[1024,128]{1,0:T(8,128)(2,1)S(1)}, u32[]{:S(2)}, u32[]{:S(2)}) collective-permute-start(bf16[1024,128]{1,0:T(8,128)(2,1)S(1)} %slice.22), channel_id=1, source_target_pairs={{0,16},{16,32},{32,48},{48,64},{64,80},{80,96},{96,112},{112,0},{1... | collective-permute-start | bytes 786440 | tf_op jit(solution)/shard_map/ppermute | solution.py:364
  77.2 1.4 %collective-permute-start.9 = (bf16[1024,128]{1,0:T(8,128)(2,1)S(1)}, bf16[1024,128]{1,0:T(8,128)(2,1)S(1)}, u32[]{:S(2)}, u32[]{:S(2)}) collective-permute-start(bf16[1024,128]{1,0:T(8,128)(2,1)S(1)} %slice.23), channel_id=1, source_target_pairs={{0,112},{16,0},{32,16},{48,32},{64,48},{80,64},{96,80},{112,96},{1... | collective-permute-start | bytes 786440 | tf_op jit(solution)/shard_map/ppermute | solution.py:365
  78.5 0.0 copy-done.3
  78.5 5.4 %shard_map.147 = (f32[2,1,1024]{2,1,0:T(1,128)S(1)}, f32[2,1,1024]{2,1,0:T(1,128)S(1)}, f32[2,128,1024]{2,1,0:T(8,128)S(1)}) custom-call(s32[5]{0:T(128)S(1)} %get-tuple-element.62.refs_0_, bf16[2048,128]{1,0:T(8,128)(2,1)S(1)} %collective-permute-done.6.refs_1_, bf16[2048,128]{1,0:T(8,128)(2,1)S(1)} %collective-permute-done.7.refs_2_, ...), custom_call_target="tpu_custom_call" | custom-call | flops 4294967296 | bytes 1048576 | tf_op jit(solution)/shard_map/pallas_call | solution.py:225
  83.9 1.0 copy-done
  84.9 9.4 %collective-permute-done.8.refs_1_ = bf16[1024,128]{1,0:T(8,128)(2,1)S(1)} collective-permute-done((bf16[1024,128]{1,0:T(8,128)(2,1)S(1)}, bf16[1024,128]{1,0:T(8,128)(2,1)S(1)}, u32[]{:S(2)}, u32[]{:S(2)}) %collective-permute-start.8) | collective-permute-done | bytes 262176 | tf_op jit(solution)/shard_map/ppermute | solution.py:364
  94.3 0.0 collective-permute-done.9.refs_2_
  94.3 0.0 all-to-all-done.2.refs_4_
  94.3 1.2 %copy-done.1 = f32[2,128,1024]{2,1,0:T(8,128)S(1)} copy-done((f32[2,128,1024]{2,1,0:T(8,128)S(1)}, f32[2,128,1024]{2,1,0:T(8,128)}, u32[]{:S(2)}) %copy-start.1) | copy-done | bytes 1048600
  95.5 7.1 %shard_map.148 = (f32[64,2048]{1,0:T(8,128)S(1)}, bf16[64,2048]{1,0:T(8,128)(2,1)S(1)}, f32[16,128]{1,0:T(8,128)S(1)}) custom-call(s32[3]{0:T(128)S(1)} %pad_add_fusion.refs_0_, bf16[1024,128]{1,0:T(8,128)(2,1)S(1)} %collective-permute-done.8.refs_1_, bf16[1024,128]{1,0:T(8,128)(2,1)S(1)} %collective-permute-done.9.refs_2_, ...), custom_call_target="tpu_custom_call" | custom-call | flops 4294967296 | bytes 1048576 | tf_op jit(solution)/shard_map/pallas_call | solution.py:225
  102.6 2.4 %collective-permute-start.10 = (bf16[64,2048]{1,0:T(8,128)(2,1)S(1)}, bf16[64,2048]{1,0:T(8,128)(2,1)S(1)}, u32[]{:S(2)}, u32[]{:S(2)}) collective-permute-start(bf16[64,2048]{1,0:T(8,128)(2,1)S(1)} %get-tuple-element.49), channel_id=1, source_target_pairs={{0,8},{8,0},{1,9},{9,1},{2,10},{10,2},{3,11},{11,3},{4,12},{12,4},... | collective-permute-start | bytes 786440 | tf_op jit(solution)/shard_map/ppermute | solution.py:379
  105.1 0.1 collective-permute-start.11
  105.2 1.1 collective-permute-done.11.theirs_ref
  106.2 0.0 collective-permute-done.10.got_ref
  106.2 1.2 %shard_map.149 = bf16[64,2048]{1,0:T(8,128)(2,1)} custom-call(f32[64,2048]{1,0:T(8,128)S(1)} %get-tuple-element.48.keep_ref, bf16[64,2048]{1,0:T(8,128)(2,1)S(1)} %collective-permute-done.10.got_ref, f32[16,128]{1,0:T(8,128)S(1)} %get-tuple-element.50.mine_ref, f32[16,128]{1,0:T(8,128)S(1)} %collective-permute-done.11.theirs_ref), custom_call_target="tpu_custom_call" | custom-call | tf_op jit(solution)/shard_map/pallas_call | solution.py:258
  (24 shorter events, 0.3 us)
Async XLA Ops:
  1.7 7.6 %copy-start.4 = (bf16[512,128]{1,0:T(8,128)(2,1)S(1)}, bf16[512,128]{1,0:T(8,128)(2,1)}, u32[]{:S(2)}) copy-start(bf16[512,128]{1,0:T(8,128)(2,1)} %param.18) | copy-start | bytes 393220
  1.7 7.6 %copy-start.5 = (bf16[512,128]{1,0:T(8,128)(2,1)S(1)}, bf16[512,128]{1,0:T(8,128)(2,1)}, u32[]{:S(2)}) copy-start(bf16[512,128]{1,0:T(8,128)(2,1)} %param.19) | copy-start | bytes 393220
  1.7 15.6 %all-to-all-start = ((bf16[8,8,2304]{2,0,1:T(8,128)(2,1)}), bf16[8,8,2304]{2,0,1:T(8,128)(2,1)S(1)}, u32[]{:S(2)}, u32[]{:S(2)}) async-start(bf16[8,8,2304]{2,0,1:T(8,128)(2,1)} %pad_maximum_fusion), calls=%async_computation | async-start | bytes 589824 | tf_op jit(solution)/shard_map/all_to_all | solution.py:296
  9.4 18.0 %collective-permute-start = (bf16[1024,128]{1,0:T(8,128)(2,1)S(1)}, bf16[1024,128]{1,0:T(8,128)(2,1)S(1)}, u32[]{:S(2)}, u32[]{:S(2)}) collective-permute-start(bf16[1024,128]{1,0:T(8,128)(2,1)S(1)} %pad_maximum_fusion.1), channel_id=1, source_target_pairs={{0,128},{128,0},{1,129},{129,1},{2,130},{130,2},{3,131},{131,3},{4... | collective-permute-start | bytes 786440 | tf_op jit(solution)/shard_map/ppermute | solution.py:276
  9.8 0.7 copy-start.11
  10.7 0.7 copy-start.8
  10.7 0.7 copy-start.9
  10.7 0.7 copy-start.10
  18.3 16.1 %all-to-all-start.1 = ((bf16[16,8,1024]{2,1,0:T(8,128)(2,1)}), bf16[16,8,1024]{2,1,0:T(8,128)(2,1)S(1)}, u32[]{:S(2)}, u32[]{:S(2)}) async-start(bf16[16,8,1024]{2,1,0:T(8,128)(2,1)} %fusion), calls=%async_computation.1 | async-start | bytes 524288 | tf_op jit(solution)/shard_map/all_to_all | solution.py:318
  27.3 2.8 %copy-start.6 = (s32[6]{0:T(128)S(1)}, s32[6]{0:T(128)}, u32[]{:S(2)}) copy-start(s32[6]{0:T(128)} %constant.298.clone) | copy-start | bytes 76
  27.3 2.8 %copy-start.7 = (pred[6]{0:T(512)(128)(4,1)S(1)}, pred[6]{0:T(512)(128)(4,1)}, u32[]{:S(2)}) copy-start(pred[6]{0:T(512)(128)(4,1)} %constant.306) | copy-start | bytes 22
  27.4 17.6 %collective-permute-start.1 = (bf16[2048,128]{1,0:T(8,128)(2,1)S(1)}, bf16[2048,128]{1,0:T(8,128)(2,1)S(1)}, u32[]{:S(2)}, u32[]{:S(2)}) collective-permute-start(bf16[2048,128]{1,0:T(8,128)(2,1)S(1)} %constant_dynamic-update-slice_fusion.refs_1_), channel_id=1, source_target_pairs={{0,16},{16,32},{32,48},{48,64},{64,80},{80,96},{96,112},{112,0},{1... | collective-permute-start | bytes 1572872 | tf_op jit(solution)/shard_map/ppermute | solution.py:281
  28.8 16.2 %collective-permute-start.3 = (bf16[2048,128]{1,0:T(8,128)(2,1)S(1)}, bf16[2048,128]{1,0:T(8,128)(2,1)S(1)}, u32[]{:S(2)}, u32[]{:S(2)}) collective-permute-start(bf16[2048,128]{1,0:T(8,128)(2,1)S(1)} %constant_dynamic-update-slice_fusion.refs_1_), channel_id=1, source_target_pairs={{0,112},{16,0},{32,16},{48,32},{64,48},{80,64},{96,80},{112,96},{1... | collective-permute-start | bytes 1572872 | tf_op jit(solution)/shard_map/ppermute | solution.py:281
  34.4 13.3 %collective-permute-start.5 = (bf16[128,1024]{1,0:T(8,128)(2,1)S(1)}, bf16[128,1024]{1,0:T(8,128)(2,1)S(1)}, u32[]{:S(2)}, u32[]{:S(2)}) collective-permute-start(bf16[128,1024]{1,0:T(8,128)(2,1)S(1)} %bitcast.14), channel_id=1, source_target_pairs={{0,8},{8,0},{1,9},{9,1},{2,10},{10,2},{3,11},{11,3},{4,12},{12,4},... | collective-permute-start | bytes 786440 | tf_op jit(solution)/shard_map/ppermute | solution.py:319
  45.0 12.1 %collective-permute-start.2 = (bf16[2048,128]{1,0:T(8,128)(2,1)S(1)}, bf16[2048,128]{1,0:T(8,128)(2,1)S(1)}, u32[]{:S(2)}, u32[]{:S(2)}) collective-permute-start(bf16[2048,128]{1,0:T(8,128)(2,1)S(1)} %collective-permute-done.1.refs_2_), channel_id=1, source_target_pairs={{0,16},{16,32},{32,48},{48,64},{64,80},{80,96},{96,112},{112,0},{1... | collective-permute-start | bytes 1572872 | tf_op jit(solution)/shard_map/ppermute | solution.py:281
  45.0 12.1 %collective-permute-start.4 = (bf16[2048,128]{1,0:T(8,128)(2,1)S(1)}, bf16[2048,128]{1,0:T(8,128)(2,1)S(1)}, u32[]{:S(2)}, u32[]{:S(2)}) collective-permute-start(bf16[2048,128]{1,0:T(8,128)(2,1)S(1)} %collective-permute-done.3.refs_3_), channel_id=1, source_target_pairs={{0,112},{16,0},{32,16},{48,32},{64,48},{80,64},{96,80},{112,96},{1... | collective-permute-start | bytes 1572872 | tf_op jit(solution)/shard_map/ppermute | solution.py:281
  57.1 9.4 %collective-permute-start.6 = (bf16[2048,128]{1,0:T(8,128)(2,1)S(1)}, bf16[2048,128]{1,0:T(8,128)(2,1)S(1)}, u32[]{:S(2)}, u32[]{:S(2)}) collective-permute-start(bf16[2048,128]{1,0:T(8,128)(2,1)S(1)} %collective-permute-done.2.refs_1_), channel_id=1, source_target_pairs={{0,16},{16,32},{32,48},{48,64},{64,80},{80,96},{96,112},{112,0},{1... | collective-permute-start | bytes 1572872 | tf_op jit(solution)/shard_map/ppermute | solution.py:281
  57.7 8.8 %collective-permute-start.7 = (bf16[2048,128]{1,0:T(8,128)(2,1)S(1)}, bf16[2048,128]{1,0:T(8,128)(2,1)S(1)}, u32[]{:S(2)}, u32[]{:S(2)}) collective-permute-start(bf16[2048,128]{1,0:T(8,128)(2,1)S(1)} %collective-permute-done.4.refs_2_), channel_id=1, source_target_pairs={{0,112},{16,0},{32,16},{48,32},{64,48},{80,64},{96,80},{112,96},{1... | collective-permute-start | bytes 1572872 | tf_op jit(solution)/shard_map/ppermute | solution.py:281
  65.5 1.0 copy-start.2
  67.4 26.8 %all-to-all-start.2 = ((bf16[16,2,64,128]{3,2,1,0:T(8,128)(2,1)}), bf16[16,2,64,128]{3,2,1,0:T(8,128)(2,1)S(1)}, u32[]{:S(2)}, u32[]{:S(2)}) async-start(bf16[16,2,64,128]{3,2,1,0:T(8,128)(2,1)} %broadcast_in_dim.112), calls=%async_computation.2 | async-start | bytes 1048576 | tf_op jit(solution)/shard_map/all_to_all | solution.py:367
  75.4 3.2 %copy-start.3 = (f32[2,128,1024]{2,1,0:T(8,128)S(1)}, f32[2,128,1024]{2,1,0:T(8,128)}, u32[]{:S(2)}) copy-start(f32[2,128,1024]{2,1,0:T(8,128)} %copy-done.2) | copy-start | bytes 3145732
  75.7 18.6 %collective-permute-start.8 = (bf16[1024,128]{1,0:T(8,128)(2,1)S(1)}, bf16[1024,128]{1,0:T(8,128)(2,1)S(1)}, u32[]{:S(2)}, u32[]{:S(2)}) collective-permute-start(bf16[1024,128]{1,0:T(8,128)(2,1)S(1)} %slice.22), channel_id=1, source_target_pairs={{0,16},{16,32},{32,48},{48,64},{64,80},{80,96},{96,112},{112,0},{1... | collective-permute-start | bytes 786440 | tf_op jit(solution)/shard_map/ppermute | solution.py:364
  77.2 17.1 %collective-permute-start.9 = (bf16[1024,128]{1,0:T(8,128)(2,1)S(1)}, bf16[1024,128]{1,0:T(8,128)(2,1)S(1)}, u32[]{:S(2)}, u32[]{:S(2)}) collective-permute-start(bf16[1024,128]{1,0:T(8,128)(2,1)S(1)} %slice.23), channel_id=1, source_target_pairs={{0,112},{16,0},{32,16},{48,32},{64,48},{80,64},{96,80},{112,96},{1... | collective-permute-start | bytes 786440 | tf_op jit(solution)/shard_map/ppermute | solution.py:365
  83.9 1.0 copy-start
  94.3 1.2 %copy-start.1 = (f32[2,128,1024]{2,1,0:T(8,128)S(1)}, f32[2,128,1024]{2,1,0:T(8,128)}, u32[]{:S(2)}) copy-start(f32[2,128,1024]{2,1,0:T(8,128)} %copy-done) | copy-start | bytes 3145732
  102.6 3.6 %collective-permute-start.10 = (bf16[64,2048]{1,0:T(8,128)(2,1)S(1)}, bf16[64,2048]{1,0:T(8,128)(2,1)S(1)}, u32[]{:S(2)}, u32[]{:S(2)}) collective-permute-start(bf16[64,2048]{1,0:T(8,128)(2,1)S(1)} %get-tuple-element.49), channel_id=1, source_target_pairs={{0,8},{8,0},{1,9},{9,1},{2,10},{10,2},{3,11},{11,3},{4,12},{12,4},... | collective-permute-start | bytes 786440 | tf_op jit(solution)/shard_map/ppermute | solution.py:379
  105.1 1.2 %collective-permute-start.11 = (f32[16,128]{1,0:T(8,128)S(1)}, f32[16,128]{1,0:T(8,128)S(1)}, u32[]{:S(2)}, u32[]{:S(2)}) collective-permute-start(f32[16,128]{1,0:T(8,128)S(1)} %get-tuple-element.50.mine_ref), channel_id=1, source_target_pairs={{0,8},{8,0},{1,9},{9,1},{2,10},{10,2},{3,11},{11,3},{4,12},{12,4},... | collective-permute-start | bytes 24584 | tf_op jit(solution)/shard_map/ppermute | solution.py:380

commit v2 on v1

--- a/solution.py
+++ b/solution.py
@@ -37,12 +37,14 @@
         keep_ref, send_ref, lse_ref = refs[at : at + 3]
         at += 3
     else:
-        m_ref, l_ref, acc_ref = refs[at : at + 3]
+        m_ref, l_ref, acc_out = refs[at : at + 3]
         at += 3
     kbuf, vbuf, qbuf, s_even, s_odd, p_even, p_odd, sems = refs[at : at + 8]
     at += 8
+    acc_ref = refs[at]
+    at += 1
     if last:
-        m_ref, l_ref, acc_ref = refs[at : at + 3]
+        m_ref, l_ref = refs[at : at + 2]
     groups = heads // GROUP
     wide = GROUP * rows
     plen = info[0]
@@ -75,6 +77,9 @@
         two.start()
 
     used = visit(begin)
+    if not first:
+        fetch = pltpu.make_async_copy(acc_in, acc_ref, sems.at[n_cached])
+        fetch.start()
 
     eye = (
         lax.broadcasted_iota(jnp.int32, (rows, HEAD_SIZE), 0) == lax.broadcasted_iota(jnp.int32, (rows, HEAD_SIZE), 1)
@@ -109,7 +114,7 @@
     else:
         m_ref[...] = m_in[...]
         l_ref[...] = l_in[...]
-        acc_ref[...] = acc_in[...]
+        fetch.wait()
 
     def finish(i, slot):
         one, two = copies(i, slot)
@@ -167,6 +172,10 @@
     for j, span in enumerate(spans):
         acc_ref[g0, :, span] = acc_ref[g0, :, span] * old[j] + pv(b0, p_odd[:, span])
 
+    if not last:
+        store = pltpu.make_async_copy(acc_ref, acc_out, sems.at[n_cached])
+        store.start()
+        store.wait()
     if last:
         half = rows // 2
         for g in range(groups):
@@ -196,7 +205,7 @@
         specs += [vm, vm]
     if not first:
         args += list(state)
-        specs += [vm] * 3
+        specs += [vm, vm, pl.BlockSpec(memory_space=pl.ANY)]
     states = [
         ((groups, 1, wide), f32),
         ((groups, 1, wide), f32),
@@ -218,15 +227,16 @@
         pltpu.VMEM((BLOCK, wide), f32),
         pltpu.VMEM((BLOCK, wide), bf16),
         pltpu.VMEM((BLOCK, wide), bf16),
-        pltpu.SemaphoreType.DMA((max(n_cached, 1),)),
+        pltpu.SemaphoreType.DMA((n_cached + 1,)),
+        pltpu.VMEM(*states[2]),
     ]
     if last:
-        scratch += [pltpu.VMEM(s, d) for s, d in states]
+        scratch += [pltpu.VMEM(s, d) for s, d in states[:2]]
     return pl.pallas_call(
         functools.partial(attend_kernel, places, len(arrays), fresh is not None, first, last, rows, heads),
         out_shape=outs,
         in_specs=specs,
-        out_specs=[vm] * 3,
+        out_specs=[vm, vm, vm if last else pl.BlockSpec(memory_space=pl.ANY)],
         scratch_shapes=scratch,
         compiler_params=pltpu.CompilerParams(vmem_limit_bytes=24 * 2**20),
         cost_estimate=pl.CostEstimate(
@@ -359,13 +369,15 @@
     state = attend(first_info, [both, up1, down1], near, queries, heads)
     up2, down2, state = lax.optimization_barrier((up2, down2, state))
     up3, down3 = hop(up2, down2)
-    state = attend(info_of(around(2)), [up2, down2], pair, queries, heads, state=state)
-    up3, down3, fresh, state = lax.optimization_barrier((up3, down3, fresh, state))
+    second_info = info_of(around(2))
+    state = attend(second_info, [up2, down2], pair, queries, heads, state=state)
+    fresh, state = lax.optimization_barrier((fresh, state))
     up4 = lax.ppermute(up3[:two], "z", up)
     down4 = lax.ppermute(down3[two:], "z", down)
     fresh = jnp.broadcast_to(fresh, (chips, 2, rows, HEAD_SIZE))
     fresh = lax.all_to_all(fresh, ("x", "z"), split_axis=0, concat_axis=0, tiled=True)
-    state = attend(info_of(around(3)), [up3, down3], pair, queries, heads, state=state)
+    third_info = info_of(around(3))
+    state = attend(third_info, [up3, down3], pair, queries, heads, state=state)
     keep, give, lse = attend(
         info_of([(0, 4), (1, 4)]),
         [up4, down4],

time: 109 us -> 117 us (1.073)
  waiting for transfers between devices: 24.5 us -> 35.1 us
  starting transfers between devices: 44.2 us -> 42.1 us
    ppermute x6, waiting for transfers between devices: 3.99 us -> 24.2 us  [hop(): return (lax.ppermute(above, 'z', up), lax.ppermute(below, 'z', down))]
    ppermute x1, waiting for transfers between devices: 9.38 us -> 0.01 us  [step(): up4 = lax.ppermute(up3[:two], 'z', up)]
    all_to_all x1, starting transfers between devices: 7.9 us -> 3.88 us  [step(): lax.all_to_all(fresh, ('x', 'z'), split_axis=0, concat_axis=0, tiled=True)]
    ppermute x1, starting transfers between devices: 2.43 us -> 4.12 us  [step(): got = lax.ppermute(give, 'c', swap)]
    ppermute x1, starting transfers between devices: 1.44 us -> 0.08 us  [step(): up4 = lax.ppermute(up3[:two], 'z', up)]
    ppermute x1, starting transfers between devices: 1.39 us -> 2.73 us  [step(): down4 = lax.ppermute(down3[two:], 'z', down)]
  transfers between devices with their start and end apart: 15 -> 15, of which waited for: 5 -> 5; matrix products, arithmetic and copies ran while one was open for 2% -> 3% of each run, Pallas kernels for 19% -> 13%
where the time goes in v2:
time: 117 us; the launch traced here: 116 us
  starting transfers between devices  42.1 us (36%)
  waiting for transfers between devices  35.1 us (30%)
  Pallas kernels  28.4 us (24%)
  local copies, waits for them, and re-layouts  4.65 us (4%)
  other arithmetic  2.68 us (2%)
  matrix products  2.27 us (2%)
    pallas_call x4, Pallas kernels, attend(): pl.pallas_call(functools.partial(attend_kernel, places, len(arrays), fres...  27.2 us
    ppermute x6, waiting for transfers between devices, hop(): return (lax.ppermute(above, 'z', up), lax.ppermute(below, 'z', down))  24.2 us
    all_to_all x1, starting transfers between devices, step(): lax.all_to_all(arranged, ('x', 'z'), split_axis=0, concat_axis=0, tiled=T...  8.37 us
    ppermute x6, starting transfers between devices, hop(): return (lax.ppermute(above, 'z', up), lax.ppermute(below, 'z', down))  8.37 us
    all_to_all x1, starting transfers between devices, step(): mixed = lax.all_to_all(mixed, 'tp', split_axis=1, concat_axis=0, tiled=True)  7.6 us
    ppermute x1, starting transfers between devices, step(): peers = lax.ppermute(mine, 'c', swap)  6.47 us
    all_to_all x1, waiting for transfers between devices, step(): mixed = lax.all_to_all(mixed, 'tp', split_axis=1, concat_axis=0, tiled=True)  4.98 us
    all_to_all x1, waiting for transfers between devices, step(): lax.all_to_all(arranged, ('x', 'z'), split_axis=0, concat_axis=0, tiled=T...  4.83 us
  transfers between devices with their start and end apart: 15, of which 5 were waited for; matrix products, arithmetic and copies ran while one was open for 3% of the time, Pallas kernels for 13%

profile of v2, /device:TPU:1, one launch (start us, length us, event | category | flops | bytes accessed | tf_op | source)
XLA Modules:
  0.0 116.2 jit_solution(16372516401493948486)
XLA Ops:
  0.0 1.7 %pad_maximum_fusion = bf16[8,8,2304]{2,0,1:T(8,128)(2,1)} fusion(bf16[8,8,128]{2,0,1:T(8,128)(2,1)} %bitcast.15, bf16[8,8,128]{2,0,1:T(8,128)(2,1)} %bitcast.16, bf16[8,8,2048]{2,0,1:T(8,128)(2,1)} %bitcast.13), kind=kLoop, calls=%fused_computation.7 | loop fusion | flops 884736 | bytes 589824 | tf_op jit(solution)/shard_map/concatenate | solution.py:298
  1.7 7.6 %all-to-all-start = ((bf16[8,8,2304]{2,0,1:T(8,128)(2,1)}), bf16[8,8,2304]{2,0,1:T(8,128)(2,1)S(1)}, u32[]{:S(2)}, u32[]{:S(2)}) async-start(bf16[8,8,2304]{2,0,1:T(8,128)(2,1)} %pad_maximum_fusion), calls=%async_computation | async-start | bytes 589824 | tf_op jit(solution)/shard_map/all_to_all | solution.py:306
  9.3 0.0 copy-done.4
  9.3 0.0 copy-done.5
  9.4 0.4 collective-permute-start
  9.8 0.0 copy-start.11
  9.9 0.6 copy-done.11
  10.5 0.1 select_reduce_fusion.2
  10.6 0.1 select_reduce_fusion
  10.7 0.0 copy-start.9
  10.7 0.0 copy-start.10
  11.4 0.0 copy-start.6
  11.4 0.0 copy-start.7
  11.4 0.0 copy-start.8
  11.5 0.6 copy-done.6
  12.1 0.0 copy-done.7
  12.1 0.0 copy-done.8
  12.1 0.1 pad_add_fusion.1.refs_0_
  12.2 0.1 fusion.9
  12.3 5.0 %all-to-all-done = bf16[8,8,2304]{2,0,1:T(8,128)(2,1)S(1)} async-done(((bf16[8,8,2304]{2,0,1:T(8,128)(2,1)}), bf16[8,8,2304]{2,0,1:T(8,128)(2,1)S(1)}, u32[]{:S(2)}, u32[]{:S(2)}) %all-to-all-start) | async-done | bytes 294944 | tf_op jit(solution)/shard_map/all_to_all | solution.py:306
  17.3 1.0 fusion
  18.3 8.4 %all-to-all-start.1 = ((bf16[16,8,1024]{2,1,0:T(8,128)(2,1)}), bf16[16,8,1024]{2,1,0:T(8,128)(2,1)}, u32[]{:S(2)}, u32[]{:S(2)}) async-start(bf16[16,8,1024]{2,1,0:T(8,128)(2,1)} %fusion), calls=%async_computation.1 | async-start | bytes 524288 | tf_op jit(solution)/shard_map/all_to_all | solution.py:328
  26.7 0.1 pad_add_fusion.2.refs_0_
  26.8 0.0 collective-permute-done
  26.8 1.4 %collective-permute-start.1 = (bf16[2048,128]{1,0:T(8,128)(2,1)S(1)}, bf16[2048,128]{1,0:T(8,128)(2,1)S(1)}, u32[]{:S(2)}, u32[]{:S(2)}) collective-permute-start(bf16[2048,128]{1,0:T(8,128)(2,1)S(1)} %constant_dynamic-update-slice_fusion.refs_1_), channel_id=1, source_target_pairs={{0,16},{16,32},{32,48},{48,64},{64,80},{80,96},{96,112},{112,0},{1... | collective-permute-start | bytes 1572872 | tf_op jit(solution)/shard_map/ppermute | solution.py:291
  28.2 1.4 %collective-permute-start.3 = (bf16[2048,128]{1,0:T(8,128)(2,1)S(1)}, bf16[2048,128]{1,0:T(8,128)(2,1)S(1)}, u32[]{:S(2)}, u32[]{:S(2)}) collective-permute-start(bf16[2048,128]{1,0:T(8,128)(2,1)S(1)} %constant_dynamic-update-slice_fusion.refs_1_), channel_id=1, source_target_pairs={{0,112},{16,0},{32,16},{48,32},{64,48},{80,64},{96,80},{112,96},{1... | collective-permute-start | bytes 1572872 | tf_op jit(solution)/shard_map/ppermute | solution.py:291
  29.6 0.1 pad_add_fusion.3.refs_0_
  29.7 4.8 %all-to-all-done.1 = bf16[16,8,1024]{2,1,0:T(8,128)(2,1)} async-done(((bf16[16,8,1024]{2,1,0:T(8,128)(2,1)}), bf16[16,8,1024]{2,1,0:T(8,128)(2,1)}, u32[]{:S(2)}, u32[]{:S(2)}) %all-to-all-start.1) | async-done | bytes 262176 | tf_op jit(solution)/shard_map/all_to_all | solution.py:328
  34.5 6.5 %collective-permute-start.5 = (bf16[128,1024]{1,0:T(8,128)(2,1)}, bf16[128,1024]{1,0:T(8,128)(2,1)S(1)}, u32[]{:S(2)}, u32[]{:S(2)}) collective-permute-start(bf16[128,1024]{1,0:T(8,128)(2,1)} %bitcast.7), channel_id=1, source_target_pairs={{0,8},{8,0},{1,9},{9,1},{2,10},{10,2},{3,11},{11,3},{4,12},{12,4},... | collective-permute-start | bytes 786440 | tf_op jit(solution)/shard_map/ppermute | solution.py:329
  41.0 4.0 %collective-permute-done.1.refs_2_ = bf16[2048,128]{1,0:T(8,128)(2,1)S(1)} collective-permute-done((bf16[2048,128]{1,0:T(8,128)(2,1)S(1)}, bf16[2048,128]{1,0:T(8,128)(2,1)S(1)}, u32[]{:S(2)}, u32[]{:S(2)}) %collective-permute-start.1) | collective-permute-done | bytes 524320 | tf_op jit(solution)/shard_map/ppermute | solution.py:291
  45.0 0.0 collective-permute-start.2
  45.0 0.0 collective-permute-done.3.refs_3_
  45.0 2.7 %collective-permute-start.4 = (bf16[2048,128]{1,0:T(8,128)(2,1)S(1)}, bf16[2048,128]{1,0:T(8,128)(2,1)S(1)}, u32[]{:S(2)}, u32[]{:S(2)}) collective-permute-start(bf16[2048,128]{1,0:T(8,128)(2,1)S(1)} %collective-permute-done.3.refs_3_), channel_id=1, source_target_pairs={{0,112},{16,0},{32,16},{48,32},{64,48},{80,64},{96,80},{112,96},{1... | collective-permute-start | bytes 1572872 | tf_op jit(solution)/shard_map/ppermute | solution.py:291
  47.7 0.0 collective-permute-done.5
  47.7 1.3 %convolution_convert_fusion.refs_4_.refs_3_ = bf16[256,1024]{1,0:T(8,128)(2,1)S(1)} fusion(bf16[128,1024]{1,0:T(8,128)(2,1)S(1)} %collective-permute-done.5, bf16[128,1024]{1,0:T(8,128)(2,1)} %bitcast.7, s32[256]{0:T(256)S(1)} %fusion.31), kind=kOutput, calls=%fused_computation | convolution fusion | flops 135593984 | bytes 1049600 | tf_op jit(solution)/shard_map/dot_general | solution.py:342
  49.0 9.2 %shard_map.145 = (f32[2,1,1024]{2,1,0:T(1,128)S(1)}, f32[2,1,1024]{2,1,0:T(1,128)S(1)}, f32[2,128,1024]{2,1,0:T(8,128)S(1)}) custom-call(s32[7]{0:T(128)S(1)} %pad_add_fusion.1.refs_0_, bf16[2048,128]{1,0:T(8,128)(2,1)S(1)} %constant_dynamic-update-slice_fusion.refs_1_, bf16[2048,128]{1,0:T(8,128)(2,1)S(1)} %collective-permute-done.1.refs_2_, ...), custom_call_target="tpu_custom_call" | custom-call | flops 6442450944 | bytes 1572864 | tf_op jit(solution)/shard_map/pallas_call | solution.py:235
  58.2 0.0 collective-permute-done.2.refs_1_
  58.2 0.0 collective-permute-done.4.refs_2_
  58.2 5.5 %shard_map.146 = (f32[2,1,1024]{2,1,0:T(1,128)S(1)}, f32[2,1,1024]{2,1,0:T(1,128)S(1)}, f32[2,128,1024]{2,1,0:T(8,128)S(1)}) custom-call(s32[5]{0:T(128)S(1)} %pad_add_fusion.2.refs_0_, bf16[2048,128]{1,0:T(8,128)(2,1)S(1)} %collective-permute-done.2.refs_1_, bf16[2048,128]{1,0:T(8,128)(2,1)S(1)} %collective-permute-done.4.refs_2_, ...), custom_call_target="tpu_custom_call" | custom-call | flops 4294967296 | bytes 1048576 | tf_op jit(solution)/shard_map/pallas_call | solution.py:235
  63.7 1.0 broadcast_in_dim.112
  64.7 3.9 %all-to-all-start.2 = ((bf16[16,2,64,128]{3,2,1,0:T(8,128)(2,1)}), bf16[16,2,64,128]{3,2,1,0:T(8,128)(2,1)S(1)}, u32[]{:S(2)}, u32[]{:S(2)}) async-start(bf16[16,2,64,128]{3,2,1,0:T(8,128)(2,1)} %broadcast_in_dim.112), calls=%async_computation.2 | async-start | bytes 1048576 | tf_op jit(solution)/shard_map/all_to_all | solution.py:378
  68.6 1.6 %collective-permute-start.6 = (bf16[2048,128]{1,0:T(8,128)(2,1)S(1)}, bf16[2048,128]{1,0:T(8,128)(2,1)S(1)}, u32[]{:S(2)}, u32[]{:S(2)}) collective-permute-start(bf16[2048,128]{1,0:T(8,128)(2,1)S(1)} %collective-permute-done.2.refs_1_), channel_id=1, source_target_pairs={{0,16},{16,32},{32,48},{48,64},{64,80},{80,96},{96,112},{112,0},{1... | collective-permute-start | bytes 1572872 | tf_op jit(solution)/shard_map/ppermute | solution.py:291
  70.2 0.0 copy-done.2
  70.2 1.3 %collective-permute-start.8 = (bf16[2048,128]{1,0:T(8,128)(2,1)S(1)}, bf16[2048,128]{1,0:T(8,128)(2,1)S(1)}, u32[]{:S(2)}, u32[]{:S(2)}) collective-permute-start(bf16[2048,128]{1,0:T(8,128)(2,1)S(1)} %collective-permute-done.4.refs_2_), channel_id=1, source_target_pairs={{0,112},{16,0},{32,16},{48,32},{64,48},{80,64},{96,80},{112,96},{1... | collective-permute-start | bytes 1572872 | tf_op jit(solution)/shard_map/ppermute | solution.py:291
  71.5 0.1 pad_add_fusion.refs_0_
  71.6 0.2 select_convert_fusion.refs_5_
  71.8 20.2 %collective-permute-done.6.refs_1_ = bf16[2048,128]{1,0:T(8,128)(2,1)S(1)} collective-permute-done((bf16[2048,128]{1,0:T(8,128)(2,1)S(1)}, bf16[2048,128]{1,0:T(8,128)(2,1)S(1)}, u32[]{:S(2)}, u32[]{:S(2)}) %collective-permute-start.6) | collective-permute-done | bytes 524320 | tf_op jit(solution)/shard_map/ppermute | solution.py:291
  92.0 0.1 collective-permute-start.7
  92.1 0.0 collective-permute-done.8.refs_2_
  92.2 2.7 %collective-permute-start.9 = (bf16[1024,128]{1,0:T(8,128)(2,1)S(1)}, bf16[1024,128]{1,0:T(8,128)(2,1)S(1)}, u32[]{:S(2)}, u32[]{:S(2)}) collective-permute-start(bf16[1024,128]{1,0:T(8,128)(2,1)S(1)} %slice.27), channel_id=1, source_target_pairs={{0,112},{16,0},{32,16},{48,32},{64,48},{80,64},{96,80},{112,96},{1... | collective-permute-start | bytes 786440 | tf_op jit(solution)/shard_map/ppermute | solution.py:376
  94.9 5.5 %shard_map.147 = (f32[2,1,1024]{2,1,0:T(1,128)S(1)}, f32[2,1,1024]{2,1,0:T(1,128)S(1)}, f32[2,128,1024]{2,1,0:T(8,128)S(1)}) custom-call(s32[5]{0:T(128)S(1)} %pad_add_fusion.3.refs_0_, bf16[2048,128]{1,0:T(8,128)(2,1)S(1)} %collective-permute-done.6.refs_1_, bf16[2048,128]{1,0:T(8,128)(2,1)S(1)} %collective-permute-done.8.refs_2_, ...), custom_call_target="tpu_custom_call" | custom-call | flops 4294967296 | bytes 1048576 | tf_op jit(solution)/shard_map/pallas_call | solution.py:235
  100.3 0.0 copy-start
  100.4 1.0 copy-done
  101.3 0.0 collective-permute-done.7.refs_1_
  101.3 0.0 collective-permute-done.9.refs_2_
  101.3 0.0 all-to-all-done.2.refs_4_
  101.3 0.0 copy-start.1
  101.4 1.2 %copy-done.1 = f32[2,128,1024]{2,1,0:T(8,128)S(1)} copy-done((f32[2,128,1024]{2,1,0:T(8,128)S(1)}, f32[2,128,1024]{2,1,0:T(8,128)}, u32[]{:S(2)}) %copy-start.1) | copy-done | bytes 1048600
  102.6 7.1 %shard_map.148 = (f32[64,2048]{1,0:T(8,128)S(1)}, bf16[64,2048]{1,0:T(8,128)(2,1)S(1)}, f32[16,128]{1,0:T(8,128)S(1)}) custom-call(s32[3]{0:T(128)S(1)} %pad_add_fusion.refs_0_, bf16[1024,128]{1,0:T(8,128)(2,1)S(1)} %collective-permute-done.7.refs_1_, bf16[1024,128]{1,0:T(8,128)(2,1)S(1)} %collective-permute-done.9.refs_2_, ...), custom_call_target="tpu_custom_call" | custom-call | flops 4294967296 | bytes 1048576 | tf_op jit(solution)/shard_map/pallas_call | solution.py:235
  109.7 4.1 %collective-permute-start.10 = (bf16[64,2048]{1,0:T(8,128)(2,1)S(1)}, bf16[64,2048]{1,0:T(8,128)(2,1)S(1)}, u32[]{:S(2)}, u32[]{:S(2)}) collective-permute-start(bf16[64,2048]{1,0:T(8,128)(2,1)S(1)} %get-tuple-element.45), channel_id=1, source_target_pairs={{0,8},{8,0},{1,9},{9,1},{2,10},{10,2},{3,11},{11,3},{4,12},{12,4},... | collective-permute-start | bytes 786440 | tf_op jit(solution)/shard_map/ppermute | solution.py:391
  113.8 0.1 collective-permute-start.11
  113.9 1.1 collective-permute-done.11.theirs_ref
  115.0 0.0 collective-permute-done.10.got_ref
  115.0 1.2 %shard_map.149 = bf16[64,2048]{1,0:T(8,128)(2,1)} custom-call(f32[64,2048]{1,0:T(8,128)S(1)} %get-tuple-element.44.keep_ref, bf16[64,2048]{1,0:T(8,128)(2,1)S(1)} %collective-permute-done.10.got_ref, f32[16,128]{1,0:T(8,128)S(1)} %get-tuple-element.46.mine_ref, f32[16,128]{1,0:T(8,128)S(1)} %collective-permute-done.11.theirs_ref), custom_call_target="tpu_custom_call" | custom-call | tf_op jit(solution)/shard_map/pallas_call | solution.py:268
  (25 shorter events, 0.3 us)
Async XLA Ops:
  1.7 7.6 %copy-start.4 = (bf16[512,128]{1,0:T(8,128)(2,1)S(1)}, bf16[512,128]{1,0:T(8,128)(2,1)}, u32[]{:S(2)}) copy-start(bf16[512,128]{1,0:T(8,128)(2,1)} %param.18) | copy-start | bytes 393220
  1.7 7.6 %copy-start.5 = (bf16[512,128]{1,0:T(8,128)(2,1)S(1)}, bf16[512,128]{1,0:T(8,128)(2,1)}, u32[]{:S(2)}) copy-start(bf16[512,128]{1,0:T(8,128)(2,1)} %param.19) | copy-start | bytes 393220
  1.7 15.6 %all-to-all-start = ((bf16[8,8,2304]{2,0,1:T(8,128)(2,1)}), bf16[8,8,2304]{2,0,1:T(8,128)(2,1)S(1)}, u32[]{:S(2)}, u32[]{:S(2)}) async-start(bf16[8,8,2304]{2,0,1:T(8,128)(2,1)} %pad_maximum_fusion), calls=%async_computation | async-start | bytes 589824 | tf_op jit(solution)/shard_map/all_to_all | solution.py:306
  9.4 17.4 %collective-permute-start = (bf16[1024,128]{1,0:T(8,128)(2,1)S(1)}, bf16[1024,128]{1,0:T(8,128)(2,1)S(1)}, u32[]{:S(2)}, u32[]{:S(2)}) collective-permute-start(bf16[1024,128]{1,0:T(8,128)(2,1)S(1)} %pad_maximum_fusion.1), channel_id=1, source_target_pairs={{0,128},{128,0},{1,129},{129,1},{2,130},{130,2},{3,131},{131,3},{4... | collective-permute-start | bytes 786440 | tf_op jit(solution)/shard_map/ppermute | solution.py:286
  9.8 0.7 copy-start.11
  10.7 0.7 copy-start.9
  10.7 0.7 copy-start.10
  11.4 0.7 copy-start.6
  11.4 0.7 copy-start.7
  11.4 0.7 copy-start.8
  18.3 16.2 %all-to-all-start.1 = ((bf16[16,8,1024]{2,1,0:T(8,128)(2,1)}), bf16[16,8,1024]{2,1,0:T(8,128)(2,1)}, u32[]{:S(2)}, u32[]{:S(2)}) async-start(bf16[16,8,1024]{2,1,0:T(8,128)(2,1)} %fusion), calls=%async_computation.1 | async-start | bytes 524288 | tf_op jit(solution)/shard_map/all_to_all | solution.py:328
  26.8 18.2 %collective-permute-start.1 = (bf16[2048,128]{1,0:T(8,128)(2,1)S(1)}, bf16[2048,128]{1,0:T(8,128)(2,1)S(1)}, u32[]{:S(2)}, u32[]{:S(2)}) collective-permute-start(bf16[2048,128]{1,0:T(8,128)(2,1)S(1)} %constant_dynamic-update-slice_fusion.refs_1_), channel_id=1, source_target_pairs={{0,16},{16,32},{32,48},{48,64},{64,80},{80,96},{96,112},{112,0},{1... | collective-permute-start | bytes 1572872 | tf_op jit(solution)/shard_map/ppermute | solution.py:291
  28.2 16.8 %collective-permute-start.3 = (bf16[2048,128]{1,0:T(8,128)(2,1)S(1)}, bf16[2048,128]{1,0:T(8,128)(2,1)S(1)}, u32[]{:S(2)}, u32[]{:S(2)}) collective-permute-start(bf16[2048,128]{1,0:T(8,128)(2,1)S(1)} %constant_dynamic-update-slice_fusion.refs_1_), channel_id=1, source_target_pairs={{0,112},{16,0},{32,16},{48,32},{64,48},{80,64},{96,80},{112,96},{1... | collective-permute-start | bytes 1572872 | tf_op jit(solution)/shard_map/ppermute | solution.py:291
  34.5 13.2 %collective-permute-start.5 = (bf16[128,1024]{1,0:T(8,128)(2,1)}, bf16[128,1024]{1,0:T(8,128)(2,1)S(1)}, u32[]{:S(2)}, u32[]{:S(2)}) collective-permute-start(bf16[128,1024]{1,0:T(8,128)(2,1)} %bitcast.7), channel_id=1, source_target_pairs={{0,8},{8,0},{1,9},{9,1},{2,10},{10,2},{3,11},{11,3},{4,12},{12,4},... | collective-permute-start | bytes 786440 | tf_op jit(solution)/shard_map/ppermute | solution.py:329
  45.0 13.1 %collective-permute-start.2 = (bf16[2048,128]{1,0:T(8,128)(2,1)S(1)}, bf16[2048,128]{1,0:T(8,128)(2,1)S(1)}, u32[]{:S(2)}, u32[]{:S(2)}) collective-permute-start(bf16[2048,128]{1,0:T(8,128)(2,1)S(1)} %collective-permute-done.1.refs_2_), channel_id=1, source_target_pairs={{0,16},{16,32},{32,48},{48,64},{64,80},{80,96},{96,112},{112,0},{1... | collective-permute-start | bytes 1572872 | tf_op jit(solution)/shard_map/ppermute | solution.py:291
  45.0 13.2 %collective-permute-start.4 = (bf16[2048,128]{1,0:T(8,128)(2,1)S(1)}, bf16[2048,128]{1,0:T(8,128)(2,1)S(1)}, u32[]{:S(2)}, u32[]{:S(2)}) collective-permute-start(bf16[2048,128]{1,0:T(8,128)(2,1)S(1)} %collective-permute-done.3.refs_3_), channel_id=1, source_target_pairs={{0,112},{16,0},{32,16},{48,32},{64,48},{80,64},{96,80},{112,96},{1... | collective-permute-start | bytes 1572872 | tf_op jit(solution)/shard_map/ppermute | solution.py:291
  63.7 6.6 %copy-start.2 = (f32[2,128,1024]{2,1,0:T(8,128)}, f32[2,128,1024]{2,1,0:T(8,128)S(1)}, u32[]{:S(2)}) copy-start(f32[2,128,1024]{2,1,0:T(8,128)S(1)} %get-tuple-element.40.refs_6_) | copy-start | bytes 3145732
  64.7 36.6 %all-to-all-start.2 = ((bf16[16,2,64,128]{3,2,1,0:T(8,128)(2,1)}), bf16[16,2,64,128]{3,2,1,0:T(8,128)(2,1)S(1)}, u32[]{:S(2)}, u32[]{:S(2)}) async-start(bf16[16,2,64,128]{3,2,1,0:T(8,128)(2,1)} %broadcast_in_dim.112), calls=%async_computation.2 | async-start | bytes 1048576 | tf_op jit(solution)/shard_map/all_to_all | solution.py:378
  68.6 23.4 %collective-permute-start.6 = (bf16[2048,128]{1,0:T(8,128)(2,1)S(1)}, bf16[2048,128]{1,0:T(8,128)(2,1)S(1)}, u32[]{:S(2)}, u32[]{:S(2)}) collective-permute-start(bf16[2048,128]{1,0:T(8,128)(2,1)S(1)} %collective-permute-done.2.refs_1_), channel_id=1, source_target_pairs={{0,16},{16,32},{32,48},{48,64},{64,80},{80,96},{96,112},{112,0},{1... | collective-permute-start | bytes 1572872 | tf_op jit(solution)/shard_map/ppermute | solution.py:291
  70.2 21.9 %collective-permute-start.8 = (bf16[2048,128]{1,0:T(8,128)(2,1)S(1)}, bf16[2048,128]{1,0:T(8,128)(2,1)S(1)}, u32[]{:S(2)}, u32[]{:S(2)}) collective-permute-start(bf16[2048,128]{1,0:T(8,128)(2,1)S(1)} %collective-permute-done.4.refs_2_), channel_id=1, source_target_pairs={{0,112},{16,0},{32,16},{48,32},{64,48},{80,64},{96,80},{112,96},{1... | collective-permute-start | bytes 1572872 | tf_op jit(solution)/shard_map/ppermute | solution.py:291
  71.5 23.3 %copy-start.3 = (f32[2,128,1024]{2,1,0:T(8,128)S(1)}, f32[2,128,1024]{2,1,0:T(8,128)}, u32[]{:S(2)}) copy-start(f32[2,128,1024]{2,1,0:T(8,128)} %copy-done.2) | copy-start | bytes 3145732
  92.0 9.3 %collective-permute-start.7 = (bf16[1024,128]{1,0:T(8,128)(2,1)S(1)}, bf16[1024,128]{1,0:T(8,128)(2,1)S(1)}, u32[]{:S(2)}, u32[]{:S(2)}) collective-permute-start(bf16[1024,128]{1,0:T(8,128)(2,1)S(1)} %slice.26), channel_id=1, source_target_pairs={{0,16},{16,32},{32,48},{48,64},{64,80},{80,96},{96,112},{112,0},{1... | collective-permute-start | bytes 786440 | tf_op jit(solution)/shard_map/ppermute | solution.py:375
  92.2 9.2 %collective-permute-start.9 = (bf16[1024,128]{1,0:T(8,128)(2,1)S(1)}, bf16[1024,128]{1,0:T(8,128)(2,1)S(1)}, u32[]{:S(2)}, u32[]{:S(2)}) collective-permute-start(bf16[1024,128]{1,0:T(8,128)(2,1)S(1)} %slice.27), channel_id=1, source_target_pairs={{0,112},{16,0},{32,16},{48,32},{64,48},{80,64},{96,80},{112,96},{1... | collective-permute-start | bytes 786440 | tf_op jit(solution)/shard_map/ppermute | solution.py:376
  100.3 1.0 copy-start
  101.3 1.2 %copy-start.1 = (f32[2,128,1024]{2,1,0:T(8,128)S(1)}, f32[2,128,1024]{2,1,0:T(8,128)}, u32[]{:S(2)}) copy-start(f32[2,128,1024]{2,1,0:T(8,128)} %copy-done) | copy-start | bytes 3145732
  109.7 5.3 %collective-permute-start.10 = (bf16[64,2048]{1,0:T(8,128)(2,1)S(1)}, bf16[64,2048]{1,0:T(8,128)(2,1)S(1)}, u32[]{:S(2)}, u32[]{:S(2)}) collective-permute-start(bf16[64,2048]{1,0:T(8,128)(2,1)S(1)} %get-tuple-element.45), channel_id=1, source_target_pairs={{0,8},{8,0},{1,9},{9,1},{2,10},{10,2},{3,11},{11,3},{4,12},{12,4},... | collective-permute-start | bytes 786440 | tf_op jit(solution)/shard_map/ppermute | solution.py:391
  113.8 1.2 %collective-permute-start.11 = (f32[16,128]{1,0:T(8,128)S(1)}, f32[16,128]{1,0:T(8,128)S(1)}, u32[]{:S(2)}, u32[]{:S(2)}) collective-permute-start(f32[16,128]{1,0:T(8,128)S(1)} %get-tuple-element.46.mine_ref), channel_id=1, source_target_pairs={{0,8},{8,0},{1,9},{9,1},{2,10},{10,2},{3,11},{11,3},{4,12},{12,4},... | collective-permute-start | bytes 24584 | tf_op jit(solution)/shard_map/ppermute | solution.py:392

commit v3 on v2

--- a/solution.py
+++ b/solution.py
@@ -28,8 +28,8 @@
     q_ref = refs[at]
     at += 1
     if has_fresh:
-        fresh_ref, fresh_mask = refs[at : at + 2]
-        at += 2
+        fresh_refs, fresh_mask = refs[at : at + 2], refs[at + 2]
+        at += 3
     if not first:
         m_in, l_in, acc_in = refs[at : at + 3]
         at += 3
@@ -99,13 +99,14 @@
 
     visit(bias)
     if has_fresh:
-        sources, per = fresh_ref.shape[0], fresh_ref.shape[2]
+        sources, _, per, _ = fresh_refs[0].shape
         count = sources * per
-        base = pl.multiple_of(used * BLOCK, BLOCK)
-        kbuf[pl.ds(base, count), pl.ds(0, HEAD_SIZE)] = fresh_ref[:, 0].reshape(count, HEAD_SIZE)
-        vbuf[pl.ds(base, count), :] = fresh_ref[:, 1].reshape(count, HEAD_SIZE)
-        kbuf[pl.ds(base, count), pl.ds(HEAD_SIZE, HEAD_SIZE)] = fresh_mask[...]
-        used = used + count // BLOCK
+        for n, ref in enumerate(fresh_refs):
+            base = pl.multiple_of((used + n * count // BLOCK) * BLOCK, BLOCK)
+            kbuf[pl.ds(base, count), pl.ds(0, HEAD_SIZE)] = ref[:, 0].reshape(count, HEAD_SIZE)
+            vbuf[pl.ds(base, count), :] = ref[:, 1].reshape(count, HEAD_SIZE)
+            kbuf[pl.ds(base, count), pl.ds(HEAD_SIZE, HEAD_SIZE)] = fresh_mask[n * count : (n + 1) * count]
+        used = used + 2 * count // BLOCK
 
     if first:
         m_ref[...] = jnp.full_like(m_ref, NEG)
@@ -196,13 +197,13 @@
     groups = heads // GROUP
     first = state is None
     n_cached = len(places)
-    slots = n_cached + (0 if fresh is None else fresh[0].shape[0] * fresh[0].shape[2] // BLOCK)
+    slots = n_cached + (0 if fresh is None else 2 * fresh[0].shape[0] * fresh[0].shape[2] // BLOCK)
     vm = pl.BlockSpec(memory_space=pltpu.VMEM)
     args = [info, *arrays, queries]
     specs = [pl.BlockSpec(memory_space=pltpu.SMEM)] + [pl.BlockSpec(memory_space=pl.ANY)] * len(arrays) + [vm]
     if fresh is not None:
         args += list(fresh)
-        specs += [vm, vm]
+        specs += [vm, vm, vm]
     if not first:
         args += list(state)
         specs += [vm, vm, pl.BlockSpec(memory_space=pl.ANY)]
@@ -348,7 +349,8 @@
         [mixed[:, width : width + HEAD_SIZE], mixed[:, width + HEAD_SIZE :]], axis=0
     ).reshape(1, 2, rows, HEAD_SIZE)
     key_id = jnp.arange(nx * nz * rows, dtype=jnp.int32)
-    key_natural = (key_id // rows * nc + c) * rows + key_id % rows
+    key_x = jnp.where(key_id // (nz * rows) == 0, x, 1 - x)
+    key_natural = ((key_x * nz + key_id // rows % nz) * nc + c) * rows + key_id % rows
     fresh_mask = jnp.where(key_natural[:, None] <= natural[None, :], 0.0, NEG).astype(bf16)
 
     slots = cached_key_rows.shape[0]
@@ -365,17 +367,18 @@
     two = 2 * slots
     near = ((0, 0), (0, two), (1, 0), (1, two), (2, 0), (2, two))
     pair = ((0, 0), (0, two), (1, 0), (1, two))
+    fresh = jnp.broadcast_to(fresh, (nz, 2, rows, HEAD_SIZE))
+    fresh = lax.all_to_all(fresh, "z", split_axis=0, concat_axis=0, tiled=True)
     first_info = info_of([(0, 0), (1, 0)] + around(1))
     state = attend(first_info, [both, up1, down1], near, queries, heads)
-    up2, down2, state = lax.optimization_barrier((up2, down2, state))
+    up2, down2, fresh, state = lax.optimization_barrier((up2, down2, fresh, state))
+    fresh_other = lax.ppermute(fresh, "x", swap)
     up3, down3 = hop(up2, down2)
     second_info = info_of(around(2))
     state = attend(second_info, [up2, down2], pair, queries, heads, state=state)
-    fresh, state = lax.optimization_barrier((fresh, state))
+    up3, down3, state = lax.optimization_barrier((up3, down3, state))
     up4 = lax.ppermute(up3[:two], "z", up)
     down4 = lax.ppermute(down3[two:], "z", down)
-    fresh = jnp.broadcast_to(fresh, (chips, 2, rows, HEAD_SIZE))
-    fresh = lax.all_to_all(fresh, ("x", "z"), split_axis=0, concat_axis=0, tiled=True)
     third_info = info_of(around(3))
     state = attend(third_info, [up3, down3], pair, queries, heads, state=state)
     keep, give, lse = attend(
@@ -384,7 +387,7 @@
         ((0, 0), (1, 0)),
         queries,
         heads,
-        fresh=(fresh, fresh_mask),
+        fresh=(fresh, fresh_other, fresh_mask),
         state=state,
         last=True,
     )

time: 117 us -> 99.9 us (0.85)
  waiting for transfers between devices: 35.1 us -> 18.1 us
  local copies, waits for them, and re-layouts: 4.65 us -> 6.22 us
  starting transfers between devices: 42.1 us -> 40.7 us
    ppermute x6, waiting for transfers between devices: 24.2 us -> 7.37 us  [hop(): return (lax.ppermute(above, 'z', up), lax.ppermute(below, 'z', down))]
    unnamed x26, local copies, waits for them, and re-layouts: 3.52 us -> 5.37 us
    ppermute x1, starting transfers between devices: 4.12 us -> 2.65 us  [step(): got = lax.ppermute(give, 'c', swap)]
  transfers between devices with their start and end apart: 15 -> 16, of which waited for: 5 -> 5; matrix products, arithmetic and copies ran while one was open for 3% -> 4% of each run, Pallas kernels for 13% -> 20%
where the time goes in v3:
time: 99.9 us; the launch traced here: 99.4 us
  starting transfers between devices  40.7 us (41%)
  Pallas kernels  28.5 us (29%)
  waiting for transfers between devices  18.1 us (18%)
  local copies, waits for them, and re-layouts  6.22 us (6%)
  other arithmetic  2.6 us (3%)
  matrix products  2.27 us (2%)
    pallas_call x4, Pallas kernels, attend(): pl.pallas_call(functools.partial(attend_kernel, places, len(arrays), fres...  27.4 us
    all_to_all x1, starting transfers between devices, step(): lax.all_to_all(arranged, ('x', 'z'), split_axis=0, concat_axis=0, tiled=T...  8.32 us
    ppermute x6, starting transfers between devices, hop(): return (lax.ppermute(above, 'z', up), lax.ppermute(below, 'z', down))  8.2 us
    all_to_all x1, starting transfers between devices, step(): mixed = lax.all_to_all(mixed, 'tp', split_axis=1, concat_axis=0, tiled=True)  7.6 us
    ppermute x6, waiting for transfers between devices, hop(): return (lax.ppermute(above, 'z', up), lax.ppermute(below, 'z', down))  7.37 us
    ppermute x1, starting transfers between devices, step(): peers = lax.ppermute(mine, 'c', swap)  6.47 us
    unnamed x26, local copies, waits for them, and re-layouts  5.37 us
    all_to_all x1, waiting for transfers between devices, step(): mixed = lax.all_to_all(mixed, 'tp', split_axis=1, concat_axis=0, tiled=True)  4.88 us
  transfers between devices with their start and end apart: 16, of which 5 were waited for; matrix products, arithmetic and copies ran while one was open for 4% of the time, Pallas kernels for 20%

profile of v3, /device:TPU:1, one launch (start us, length us, event | category | flops | bytes accessed | tf_op | source)
XLA Modules:
  0.0 99.4 jit_solution(7003089443039648066)
XLA Ops:
  0.0 1.7 %pad_maximum_fusion = bf16[8,8,2304]{2,0,1:T(8,128)(2,1)} fusion(bf16[8,8,128]{2,0,1:T(8,128)(2,1)} %bitcast.16, bf16[8,8,128]{2,0,1:T(8,128)(2,1)} %bitcast.17, bf16[8,8,2048]{2,0,1:T(8,128)(2,1)} %bitcast.12), kind=kLoop, calls=%fused_computation.7 | loop fusion | flops 884736 | bytes 589824 | tf_op jit(solution)/shard_map/concatenate | solution.py:299
  1.7 7.6 %all-to-all-start = ((bf16[8,8,2304]{2,0,1:T(8,128)(2,1)}), bf16[8,8,2304]{2,0,1:T(8,128)(2,1)S(1)}, u32[]{:S(2)}, u32[]{:S(2)}) async-start(bf16[8,8,2304]{2,0,1:T(8,128)(2,1)} %pad_maximum_fusion), calls=%async_computation | async-start | bytes 589824 | tf_op jit(solution)/shard_map/all_to_all | solution.py:307
  9.3 0.0 copy-done.4
  9.3 0.0 copy-done.5
  9.4 0.4 collective-permute-start
  9.8 0.0 copy-start.11
  9.9 0.6 copy-done.11
  10.5 0.1 select_reduce_fusion.2
  10.6 0.1 select_reduce_fusion
  10.7 0.0 copy-start.9
  10.7 0.0 copy-start.10
  10.8 0.6 copy-done.9
  11.4 0.0 copy-done.10
  11.4 0.1 fusion.9
  12.2 0.2 select_convert_fusion.refs_6_
  12.4 4.9 %all-to-all-done = bf16[8,8,2304]{2,0,1:T(8,128)(2,1)S(1)} async-done(((bf16[8,8,2304]{2,0,1:T(8,128)(2,1)}), bf16[8,8,2304]{2,0,1:T(8,128)(2,1)S(1)}, u32[]{:S(2)}, u32[]{:S(2)}) %all-to-all-start) | async-done | bytes 294944 | tf_op jit(solution)/shard_map/all_to_all | solution.py:307
  17.3 1.0 fusion
  18.3 8.3 %all-to-all-start.2 = ((bf16[16,8,1024]{2,1,0:T(8,128)(2,1)}), bf16[16,8,1024]{2,1,0:T(8,128)(2,1)S(1)}, u32[]{:S(2)}, u32[]{:S(2)}) async-start(bf16[16,8,1024]{2,1,0:T(8,128)(2,1)} %fusion), calls=%async_computation.2 | async-start | bytes 524288 | tf_op jit(solution)/shard_map/all_to_all | solution.py:329
  26.6 0.1 pad_add_fusion.1.refs_0_
  26.7 0.0 copy-start.6
  26.7 0.0 copy-start.7
  26.7 0.0 copy-start.8
  26.8 0.0 collective-permute-done
  26.8 1.4 %collective-permute-start.1 = (bf16[2048,128]{1,0:T(8,128)(2,1)S(1)}, bf16[2048,128]{1,0:T(8,128)(2,1)S(1)}, u32[]{:S(2)}, u32[]{:S(2)}) collective-permute-start(bf16[2048,128]{1,0:T(8,128)(2,1)S(1)} %constant_dynamic-update-slice_fusion.refs_1_), channel_id=1, source_target_pairs={{0,16},{16,32},{32,48},{48,64},{64,80},{80,96},{96,112},{112,0},{1... | collective-permute-start | bytes 1572872 | tf_op jit(solution)/shard_map/ppermute | solution.py:292
  28.3 1.3 %collective-permute-start.3 = (bf16[2048,128]{1,0:T(8,128)(2,1)S(1)}, bf16[2048,128]{1,0:T(8,128)(2,1)S(1)}, u32[]{:S(2)}, u32[]{:S(2)}) collective-permute-start(bf16[2048,128]{1,0:T(8,128)(2,1)S(1)} %constant_dynamic-update-slice_fusion.refs_1_), channel_id=1, source_target_pairs={{0,112},{16,0},{32,16},{48,32},{64,48},{80,64},{96,80},{112,96},{1... | collective-permute-start | bytes 1572872 | tf_op jit(solution)/shard_map/ppermute | solution.py:292
  29.6 0.0 copy-done.6
  29.6 4.8 %all-to-all-done.2 = bf16[16,8,1024]{2,1,0:T(8,128)(2,1)S(1)} async-done(((bf16[16,8,1024]{2,1,0:T(8,128)(2,1)}), bf16[16,8,1024]{2,1,0:T(8,128)(2,1)S(1)}, u32[]{:S(2)}, u32[]{:S(2)}) %all-to-all-start.2) | async-done | bytes 262176 | tf_op jit(solution)/shard_map/all_to_all | solution.py:329
  34.4 6.5 %collective-permute-start.5 = (bf16[128,1024]{1,0:T(8,128)(2,1)S(1)}, bf16[128,1024]{1,0:T(8,128)(2,1)}, u32[]{:S(2)}, u32[]{:S(2)}) collective-permute-start(bf16[128,1024]{1,0:T(8,128)(2,1)S(1)} %bitcast.13), channel_id=1, source_target_pairs={{0,8},{8,0},{1,9},{9,1},{2,10},{10,2},{3,11},{11,3},{4,12},{12,4},... | collective-permute-start | bytes 786440 | tf_op jit(solution)/shard_map/ppermute | solution.py:330
  40.9 0.8 broadcast_in_dim.111
  41.6 3.5 %all-to-all-start.1 = ((bf16[8,2,64,128]{3,2,1,0:T(8,128)(2,1)}), bf16[8,2,64,128]{3,2,1,0:T(8,128)(2,1)S(1)}, u32[]{:S(2)}, u32[]{:S(2)}) async-start(bf16[8,2,64,128]{3,2,1,0:T(8,128)(2,1)} %broadcast_in_dim.111), calls=%async_computation.1 | async-start | bytes 524288 | tf_op jit(solution)/shard_map/all_to_all | solution.py:371
  45.1 0.0 collective-permute-done.1.refs_2_
  45.1 1.5 %collective-permute-start.2 = (bf16[2048,128]{1,0:T(8,128)(2,1)S(1)}, bf16[2048,128]{1,0:T(8,128)(2,1)S(1)}, u32[]{:S(2)}, u32[]{:S(2)}) collective-permute-start(bf16[2048,128]{1,0:T(8,128)(2,1)S(1)} %collective-permute-done.1.refs_2_), channel_id=1, source_target_pairs={{0,16},{16,32},{32,48},{48,64},{64,80},{80,96},{96,112},{112,0},{1... | collective-permute-start | bytes 1572872 | tf_op jit(solution)/shard_map/ppermute | solution.py:292
  46.5 0.0 collective-permute-done.3.refs_3_
  46.6 1.3 %collective-permute-start.4 = (bf16[2048,128]{1,0:T(8,128)(2,1)S(1)}, bf16[2048,128]{1,0:T(8,128)(2,1)S(1)}, u32[]{:S(2)}, u32[]{:S(2)}) collective-permute-start(bf16[2048,128]{1,0:T(8,128)(2,1)S(1)} %collective-permute-done.3.refs_3_), channel_id=1, source_target_pairs={{0,112},{16,0},{32,16},{48,32},{64,48},{80,64},{96,80},{112,96},{1... | collective-permute-start | bytes 1572872 | tf_op jit(solution)/shard_map/ppermute | solution.py:292
  47.9 0.0 collective-permute-done.5
  47.9 1.3 %convolution_convert_fusion.refs_4_.refs_3_ = bf16[256,1024]{1,0:T(8,128)(2,1)S(1)} fusion(bf16[128,1024]{1,0:T(8,128)(2,1)} %collective-permute-done.5, bf16[128,1024]{1,0:T(8,128)(2,1)S(1)} %bitcast.14, s32[256]{0:T(256)S(1)} %fusion.34), kind=kOutput, calls=%fused_computation | convolution fusion | flops 135593984 | bytes 1049600 | tf_op jit(solution)/shard_map/dot_general | solution.py:343
  49.2 9.1 %shard_map.145 = (f32[2,1,1024]{2,1,0:T(1,128)S(1)}, f32[2,1,1024]{2,1,0:T(1,128)S(1)}, f32[2,128,1024]{2,1,0:T(8,128)S(1)}) custom-call(s32[7]{0:T(128)S(1)} %pad_add_fusion.1.refs_0_, bf16[2048,128]{1,0:T(8,128)(2,1)S(1)} %constant_dynamic-update-slice_fusion.refs_1_, bf16[2048,128]{1,0:T(8,128)(2,1)S(1)} %collective-permute-done.1.refs_2_, ...), custom_call_target="tpu_custom_call" | custom-call | flops 6442450944 | bytes 1572864 | tf_op jit(solution)/shard_map/pallas_call | solution.py:236
  58.3 0.8 copy-done
  59.1 1.0 copy-done.2
  60.1 0.0 all-to-all-done.1.refs_4_
  60.1 5.2 %collective-permute-done.2.refs_1_ = bf16[2048,128]{1,0:T(8,128)(2,1)S(1)} collective-permute-done((bf16[2048,128]{1,0:T(8,128)(2,1)S(1)}, bf16[2048,128]{1,0:T(8,128)(2,1)S(1)}, u32[]{:S(2)}, u32[]{:S(2)}) %collective-permute-start.2) | collective-permute-done | bytes 524320 | tf_op jit(solution)/shard_map/ppermute | solution.py:292
  65.3 0.0 collective-permute-done.4.refs_2_
  65.3 0.0 collective-permute-start.6
  65.3 2.7 %collective-permute-start.7 = (bf16[2048,128]{1,0:T(8,128)(2,1)S(1)}, bf16[2048,128]{1,0:T(8,128)(2,1)S(1)}, u32[]{:S(2)}, u32[]{:S(2)}) collective-permute-start(bf16[2048,128]{1,0:T(8,128)(2,1)S(1)} %collective-permute-done.4.refs_2_), channel_id=1, source_target_pairs={{0,112},{16,0},{32,16},{48,32},{64,48},{80,64},{96,80},{112,96},{1... | collective-permute-start | bytes 1572872 | tf_op jit(solution)/shard_map/ppermute | solution.py:292
  68.0 0.1 pad_add_fusion.refs_0_
  68.1 0.1 pad_add_fusion.2
  68.1 0.7 collective-permute-start.10
  68.8 1.0 %copy-done.1 = bf16[256,1024]{1,0:T(8,128)(2,1)S(1)} copy-done((bf16[256,1024]{1,0:T(8,128)(2,1)S(1)}, bf16[256,1024]{1,0:T(8,128)(2,1)}, u32[]{:S(2)}) %copy-start.1) | copy-done | bytes 524312
  69.9 1.2 %copy-done.3 = f32[2,128,1024]{2,1,0:T(8,128)S(1)} copy-done((f32[2,128,1024]{2,1,0:T(8,128)S(1)}, f32[2,128,1024]{2,1,0:T(8,128)}, u32[]{:S(2)}) %copy-start.3) | copy-done | bytes 1048600
  71.1 5.6 %shard_map.146 = (f32[2,1,1024]{2,1,0:T(1,128)S(1)}, f32[2,1,1024]{2,1,0:T(1,128)S(1)}, f32[2,128,1024]{2,1,0:T(8,128)S(1)}) custom-call(s32[5]{0:T(128)S(1)} %get-tuple-element.61.refs_0_, bf16[2048,128]{1,0:T(8,128)(2,1)S(1)} %collective-permute-done.2.refs_1_, bf16[2048,128]{1,0:T(8,128)(2,1)S(1)} %collective-permute-done.4.refs_2_, ...), custom_call_target="tpu_custom_call" | custom-call | flops 4294967296 | bytes 1048576 | tf_op jit(solution)/shard_map/pallas_call | solution.py:236
  76.7 2.2 %collective-permute-done.6.refs_1_ = bf16[2048,128]{1,0:T(8,128)(2,1)S(1)} collective-permute-done((bf16[2048,128]{1,0:T(8,128)(2,1)S(1)}, bf16[2048,128]{1,0:T(8,128)(2,1)S(1)}, u32[]{:S(2)}, u32[]{:S(2)}) %collective-permute-start.6) | collective-permute-done | bytes 524320 | tf_op jit(solution)/shard_map/ppermute | solution.py:292
  78.9 0.0 collective-permute-done.7.refs_2_
  78.9 1.1 %collective-permute-start.8 = (bf16[1024,128]{1,0:T(8,128)(2,1)S(1)}, bf16[1024,128]{1,0:T(8,128)(2,1)S(1)}, u32[]{:S(2)}, u32[]{:S(2)}) collective-permute-start(bf16[1024,128]{1,0:T(8,128)(2,1)S(1)} %slice.22), channel_id=1, source_target_pairs={{0,16},{16,32},{32,48},{48,64},{64,80},{80,96},{96,112},{112,0},{1... | collective-permute-start | bytes 786440 | tf_op jit(solution)/shard_map/ppermute | solution.py:380
  80.1 1.7 %collective-permute-start.9 = (bf16[1024,128]{1,0:T(8,128)(2,1)S(1)}, bf16[1024,128]{1,0:T(8,128)(2,1)S(1)}, u32[]{:S(2)}, u32[]{:S(2)}) collective-permute-start(bf16[1024,128]{1,0:T(8,128)(2,1)S(1)} %slice.23), channel_id=1, source_target_pairs={{0,112},{16,0},{32,16},{48,32},{64,48},{80,64},{96,80},{112,96},{1... | collective-permute-start | bytes 786440 | tf_op jit(solution)/shard_map/ppermute | solution.py:381
  81.8 5.5 %shard_map.147 = (f32[2,1,1024]{2,1,0:T(1,128)S(1)}, f32[2,1,1024]{2,1,0:T(1,128)S(1)}, f32[2,128,1024]{2,1,0:T(8,128)S(1)}) custom-call(s32[5]{0:T(128)S(1)} %get-tuple-element.62.refs_0_, bf16[2048,128]{1,0:T(8,128)(2,1)S(1)} %collective-permute-done.6.refs_1_, bf16[2048,128]{1,0:T(8,128)(2,1)S(1)} %collective-permute-done.7.refs_2_, ...), custom_call_target="tpu_custom_call" | custom-call | flops 4294967296 | bytes 1048576 | tf_op jit(solution)/shard_map/pallas_call | solution.py:236
  87.2 0.0 collective-permute-done.10.refs_5_
  87.2 0.0 collective-permute-done.8.refs_1_
  87.2 0.0 collective-permute-done.9.refs_2_
  87.3 7.1 %shard_map.148 = (f32[64,2048]{1,0:T(8,128)S(1)}, bf16[64,2048]{1,0:T(8,128)(2,1)S(1)}, f32[16,128]{1,0:T(8,128)S(1)}) custom-call(s32[3]{0:T(128)S(1)} %pad_add_fusion.refs_0_, bf16[1024,128]{1,0:T(8,128)(2,1)S(1)} %collective-permute-done.8.refs_1_, bf16[1024,128]{1,0:T(8,128)(2,1)S(1)} %collective-permute-done.9.refs_2_, bf16[256,1024]{1,0:T(8,128)(2,1)S(1)} %copy-done.1, ...), custom_call_target="tpu_custom_call" | custom-call | flops 4294967296 | bytes 1048576 | tf_op jit(solution)/shard_map/pallas_call | solution.py:236
  94.4 2.6 %collective-permute-start.11 = (bf16[64,2048]{1,0:T(8,128)(2,1)S(1)}, bf16[64,2048]{1,0:T(8,128)(2,1)S(1)}, u32[]{:S(2)}, u32[]{:S(2)}) collective-permute-start(bf16[64,2048]{1,0:T(8,128)(2,1)S(1)} %get-tuple-element.49), channel_id=1, source_target_pairs={{0,8},{8,0},{1,9},{9,1},{2,10},{10,2},{3,11},{11,3},{4,12},{12,4},... | collective-permute-start | bytes 786440 | tf_op jit(solution)/shard_map/ppermute | solution.py:394
  97.0 0.1 collective-permute-start.12
  97.1 1.1 %collective-permute-done.12.theirs_ref = f32[16,128]{1,0:T(8,128)S(1)} collective-permute-done((f32[16,128]{1,0:T(8,128)S(1)}, f32[16,128]{1,0:T(8,128)S(1)}, u32[]{:S(2)}, u32[]{:S(2)}) %collective-permute-start.12) | collective-permute-done | bytes 8224 | tf_op jit(solution)/shard_map/ppermute | solution.py:395
  98.2 0.0 collective-permute-done.11.got_ref
  98.2 1.2 %shard_map.149 = bf16[64,2048]{1,0:T(8,128)(2,1)} custom-call(f32[64,2048]{1,0:T(8,128)S(1)} %get-tuple-element.48.keep_ref, bf16[64,2048]{1,0:T(8,128)(2,1)S(1)} %collective-permute-done.11.got_ref, f32[16,128]{1,0:T(8,128)S(1)} %get-tuple-element.50.mine_ref, f32[16,128]{1,0:T(8,128)S(1)} %collective-permute-done.12.theirs_ref), custom_call_target="tpu_custom_call" | custom-call | tf_op jit(solution)/shard_map/pallas_call | solution.py:269
  (26 shorter events, 0.3 us)
Async XLA Ops:
  1.7 7.6 %copy-start.4 = (bf16[512,128]{1,0:T(8,128)(2,1)S(1)}, bf16[512,128]{1,0:T(8,128)(2,1)}, u32[]{:S(2)}) copy-start(bf16[512,128]{1,0:T(8,128)(2,1)} %param.18) | copy-start | bytes 393220
  1.7 7.6 %copy-start.5 = (bf16[512,128]{1,0:T(8,128)(2,1)S(1)}, bf16[512,128]{1,0:T(8,128)(2,1)}, u32[]{:S(2)}) copy-start(bf16[512,128]{1,0:T(8,128)(2,1)} %param.19) | copy-start | bytes 393220
  1.7 15.6 %all-to-all-start = ((bf16[8,8,2304]{2,0,1:T(8,128)(2,1)}), bf16[8,8,2304]{2,0,1:T(8,128)(2,1)S(1)}, u32[]{:S(2)}, u32[]{:S(2)}) async-start(bf16[8,8,2304]{2,0,1:T(8,128)(2,1)} %pad_maximum_fusion), calls=%async_computation | async-start | bytes 589824 | tf_op jit(solution)/shard_map/all_to_all | solution.py:307
  9.4 17.4 %collective-permute-start = (bf16[1024,128]{1,0:T(8,128)(2,1)S(1)}, bf16[1024,128]{1,0:T(8,128)(2,1)S(1)}, u32[]{:S(2)}, u32[]{:S(2)}) collective-permute-start(bf16[1024,128]{1,0:T(8,128)(2,1)S(1)} %pad_maximum_fusion.1), channel_id=1, source_target_pairs={{0,128},{128,0},{1,129},{129,1},{2,130},{130,2},{3,131},{131,3},{4... | collective-permute-start | bytes 786440 | tf_op jit(solution)/shard_map/ppermute | solution.py:287
  9.8 0.7 copy-start.11
  10.7 0.7 copy-start.9
  10.7 0.7 copy-start.10
  18.3 16.1 %all-to-all-start.2 = ((bf16[16,8,1024]{2,1,0:T(8,128)(2,1)}), bf16[16,8,1024]{2,1,0:T(8,128)(2,1)S(1)}, u32[]{:S(2)}, u32[]{:S(2)}) async-start(bf16[16,8,1024]{2,1,0:T(8,128)(2,1)} %fusion), calls=%async_computation.2 | async-start | bytes 524288 | tf_op jit(solution)/shard_map/all_to_all | solution.py:329
  26.7 2.9 %copy-start.6 = (s32[4]{0:T(128)S(1)}, s32[4]{0:T(128)}, u32[]{:S(2)}) copy-start(s32[4]{0:T(128)} %constant.320.clone) | copy-start | bytes 52
  26.7 2.8 %copy-start.7 = (s32[4]{0:T(128)S(1)}, s32[4]{0:T(128)}, u32[]{:S(2)}) copy-start(s32[4]{0:T(128)} %constant.321.clone) | copy-start | bytes 52
  26.7 2.8 %copy-start.8 = (pred[4]{0:T(512)(128)(4,1)S(1)}, pred[4]{0:T(512)(128)(4,1)}, u32[]{:S(2)}) copy-start(pred[4]{0:T(512)(128)(4,1)} %constant.327) | copy-start | bytes 16
  26.8 18.3 %collective-permute-start.1 = (bf16[2048,128]{1,0:T(8,128)(2,1)S(1)}, bf16[2048,128]{1,0:T(8,128)(2,1)S(1)}, u32[]{:S(2)}, u32[]{:S(2)}) collective-permute-start(bf16[2048,128]{1,0:T(8,128)(2,1)S(1)} %constant_dynamic-update-slice_fusion.refs_1_), channel_id=1, source_target_pairs={{0,16},{16,32},{32,48},{48,64},{64,80},{80,96},{96,112},{112,0},{1... | collective-permute-start | bytes 1572872 | tf_op jit(solution)/shard_map/ppermute | solution.py:292
  28.3 18.3 %collective-permute-start.3 = (bf16[2048,128]{1,0:T(8,128)(2,1)S(1)}, bf16[2048,128]{1,0:T(8,128)(2,1)S(1)}, u32[]{:S(2)}, u32[]{:S(2)}) collective-permute-start(bf16[2048,128]{1,0:T(8,128)(2,1)S(1)} %constant_dynamic-update-slice_fusion.refs_1_), channel_id=1, source_target_pairs={{0,112},{16,0},{32,16},{48,32},{64,48},{80,64},{96,80},{112,96},{1... | collective-permute-start | bytes 1572872 | tf_op jit(solution)/shard_map/ppermute | solution.py:292
  34.4 13.5 %collective-permute-start.5 = (bf16[128,1024]{1,0:T(8,128)(2,1)S(1)}, bf16[128,1024]{1,0:T(8,128)(2,1)}, u32[]{:S(2)}, u32[]{:S(2)}) collective-permute-start(bf16[128,1024]{1,0:T(8,128)(2,1)S(1)} %bitcast.13), channel_id=1, source_target_pairs={{0,8},{8,0},{1,9},{9,1},{2,10},{10,2},{3,11},{11,3},{4,12},{12,4},... | collective-permute-start | bytes 786440 | tf_op jit(solution)/shard_map/ppermute | solution.py:330
  41.6 18.5 %all-to-all-start.1 = ((bf16[8,2,64,128]{3,2,1,0:T(8,128)(2,1)}), bf16[8,2,64,128]{3,2,1,0:T(8,128)(2,1)S(1)}, u32[]{:S(2)}, u32[]{:S(2)}) async-start(bf16[8,2,64,128]{3,2,1,0:T(8,128)(2,1)} %broadcast_in_dim.111), calls=%async_computation.1 | async-start | bytes 524288 | tf_op jit(solution)/shard_map/all_to_all | solution.py:371
  45.1 20.2 %collective-permute-start.2 = (bf16[2048,128]{1,0:T(8,128)(2,1)S(1)}, bf16[2048,128]{1,0:T(8,128)(2,1)S(1)}, u32[]{:S(2)}, u32[]{:S(2)}) collective-permute-start(bf16[2048,128]{1,0:T(8,128)(2,1)S(1)} %collective-permute-done.1.refs_2_), channel_id=1, source_target_pairs={{0,16},{16,32},{32,48},{48,64},{64,80},{80,96},{96,112},{112,0},{1... | collective-permute-start | bytes 1572872 | tf_op jit(solution)/shard_map/ppermute | solution.py:292
  46.6 18.8 %collective-permute-start.4 = (bf16[2048,128]{1,0:T(8,128)(2,1)S(1)}, bf16[2048,128]{1,0:T(8,128)(2,1)S(1)}, u32[]{:S(2)}, u32[]{:S(2)}) collective-permute-start(bf16[2048,128]{1,0:T(8,128)(2,1)S(1)} %collective-permute-done.3.refs_3_), channel_id=1, source_target_pairs={{0,112},{16,0},{32,16},{48,32},{64,48},{80,64},{96,80},{112,96},{1... | collective-permute-start | bytes 1572872 | tf_op jit(solution)/shard_map/ppermute | solution.py:292
  58.3 0.8 copy-start
  59.1 1.0 copy-start.2
  65.3 13.6 %collective-permute-start.6 = (bf16[2048,128]{1,0:T(8,128)(2,1)S(1)}, bf16[2048,128]{1,0:T(8,128)(2,1)S(1)}, u32[]{:S(2)}, u32[]{:S(2)}) collective-permute-start(bf16[2048,128]{1,0:T(8,128)(2,1)S(1)} %collective-permute-done.2.refs_1_), channel_id=1, source_target_pairs={{0,16},{16,32},{32,48},{48,64},{64,80},{80,96},{96,112},{112,0},{1... | collective-permute-start | bytes 1572872 | tf_op jit(solution)/shard_map/ppermute | solution.py:292
  65.3 13.6 %collective-permute-start.7 = (bf16[2048,128]{1,0:T(8,128)(2,1)S(1)}, bf16[2048,128]{1,0:T(8,128)(2,1)S(1)}, u32[]{:S(2)}, u32[]{:S(2)}) collective-permute-start(bf16[2048,128]{1,0:T(8,128)(2,1)S(1)} %collective-permute-done.4.refs_2_), channel_id=1, source_target_pairs={{0,112},{16,0},{32,16},{48,32},{64,48},{80,64},{96,80},{112,96},{1... | collective-permute-start | bytes 1572872 | tf_op jit(solution)/shard_map/ppermute | solution.py:292
  68.1 19.1 %collective-permute-start.10 = (bf16[8,2,64,128]{3,2,1,0:T(8,128)(2,1)S(1)}, bf16[8,2,64,128]{3,2,1,0:T(8,128)(2,1)S(1)}, u32[]{:S(2)}, u32[]{:S(2)}) collective-permute-start(bf16[8,2,64,128]{3,2,1,0:T(8,128)(2,1)S(1)} %all-to-all-done.1.refs_4_), channel_id=1, source_target_pairs={{0,128},{128,0},{1,129},{129,1},{2,130},{130,2},{3,131},{131,3},{4... | collective-permute-start | bytes 786440 | tf_op jit(solution)/shard_map/ppermute | solution.py:375
  68.8 1.0 %copy-start.1 = (bf16[256,1024]{1,0:T(8,128)(2,1)S(1)}, bf16[256,1024]{1,0:T(8,128)(2,1)}, u32[]{:S(2)}) copy-start(bf16[256,1024]{1,0:T(8,128)(2,1)} %copy-done) | copy-start | bytes 1572868
  69.8 1.2 %copy-start.3 = (f32[2,128,1024]{2,1,0:T(8,128)S(1)}, f32[2,128,1024]{2,1,0:T(8,128)}, u32[]{:S(2)}) copy-start(f32[2,128,1024]{2,1,0:T(8,128)} %copy-done.2) | copy-start | bytes 3145732
  78.9 8.3 %collective-permute-start.8 = (bf16[1024,128]{1,0:T(8,128)(2,1)S(1)}, bf16[1024,128]{1,0:T(8,128)(2,1)S(1)}, u32[]{:S(2)}, u32[]{:S(2)}) collective-permute-start(bf16[1024,128]{1,0:T(8,128)(2,1)S(1)} %slice.22), channel_id=1, source_target_pairs={{0,16},{16,32},{32,48},{48,64},{64,80},{80,96},{96,112},{112,0},{1... | collective-permute-start | bytes 786440 | tf_op jit(solution)/shard_map/ppermute | solution.py:380
  80.1 7.2 %collective-permute-start.9 = (bf16[1024,128]{1,0:T(8,128)(2,1)S(1)}, bf16[1024,128]{1,0:T(8,128)(2,1)S(1)}, u32[]{:S(2)}, u32[]{:S(2)}) collective-permute-start(bf16[1024,128]{1,0:T(8,128)(2,1)S(1)} %slice.23), channel_id=1, source_target_pairs={{0,112},{16,0},{32,16},{48,32},{64,48},{80,64},{96,80},{112,96},{1... | collective-permute-start | bytes 786440 | tf_op jit(solution)/shard_map/ppermute | solution.py:381
  94.4 3.8 %collective-permute-start.11 = (bf16[64,2048]{1,0:T(8,128)(2,1)S(1)}, bf16[64,2048]{1,0:T(8,128)(2,1)S(1)}, u32[]{:S(2)}, u32[]{:S(2)}) collective-permute-start(bf16[64,2048]{1,0:T(8,128)(2,1)S(1)} %get-tuple-element.49), channel_id=1, source_target_pairs={{0,8},{8,0},{1,9},{9,1},{2,10},{10,2},{3,11},{11,3},{4,12},{12,4},... | collective-permute-start | bytes 786440 | tf_op jit(solution)/shard_map/ppermute | solution.py:394
  97.0 1.2 %collective-permute-start.12 = (f32[16,128]{1,0:T(8,128)S(1)}, f32[16,128]{1,0:T(8,128)S(1)}, u32[]{:S(2)}, u32[]{:S(2)}) collective-permute-start(f32[16,128]{1,0:T(8,128)S(1)} %get-tuple-element.50.mine_ref), channel_id=1, source_target_pairs={{0,8},{8,0},{1,9},{9,1},{2,10},{10,2},{3,11},{11,3},{4,12},{12,4},... | collective-permute-start | bytes 24584 | tf_op jit(solution)/shard_map/ppermute | solution.py:395
